TPU v7x, 128 devices: a whole 4x4x4 slice. The times are simulated.
128 devices in a mesh: gy: 8 (over z, y_hi), gz: 16 (over y_lo, x, core).
Axes of the slice: x: 4, y: 4 (y_hi: 2, y_lo: 2; y = y_hi * 2 + y_lo), z: 4, core: 2. Of those that a mesh axis runs over, the one named last changes fastest.
Arguments:
- fields: bfloat16 [1024, 32, 128, 64], P(None, 'gy', 'gz'), may hold values from -6 to 6
- spec_weight: float32 [32, 2, 64, 64], P('gz'), may hold values from -1.5 to 1.5
- skip_weight: bfloat16 [64, 64], replicated, may hold values from -0.75 to 0.75
- up_weight: bfloat16 [64, 256], replicated, may hold values from -0.75 to 0.75
- down_weight: bfloat16 [256, 64], replicated, may hold values from -0.375 to 0.375
- cotangent: bfloat16 [1024, 32, 128, 64], P(None, 'gy', 'gz'), may hold values from -6 to 6
Outputs:
- output: bfloat16 [1024, 32, 128, 64], P(None, 'gy', 'gz')
- grad_fields: bfloat16 [1024, 32, 128, 64], P(None, 'gy', 'gz')
- grad_spec: float32 [32, 2, 64, 64], P('gz')
- grad_skip: float32 [64, 64], replicated
- grad_up: float32 [64, 256], replicated
- grad_down: float32 [256, 64], replicated
All inputs are finite; a program needn't handle non-finite values.
Results may differ from a plain program's by a relative error of at most 0.0067.
Values sent between devices are 32-bit elements; how exact they have to be, the bound alone decides.
No kernel may reach another device: no remote copies, remote signals or barrier semaphores. Data moves between devices by JAX's collectives and lax.ppermute only.
A program may use at most 192 MiB of HBM per device.

v0:
```python
import functools
import math

import jax
import jax.numpy as jnp
from jax import lax
from jax.experimental import pallas as pl
from jax.experimental.pallas import tpu as pltpu
from jax.sharding import PartitionSpec as P

MODES = 32
BF16 = jnp.bfloat16
F32 = jnp.float32
CHUNK = 256


def sent_to_all(shard, axis):
    peers = lax.axis_size(axis)
    return lax.all_to_all(
        jnp.broadcast_to(shard[None], (peers, *shard.shape)), axis, 0, 0, tiled=True
    )


def fourier_tables(length_x, kept):
    position = jnp.arange(length_x, dtype=jnp.int32)[:, None]
    wavenum = jnp.arange(kept, dtype=jnp.int32)[None, :]
    phase = (position * wavenum % length_x).astype(F32) * (2.0 * math.pi / length_x)
    factor = 1.0 / math.sqrt(length_x)
    analysis = jnp.concatenate([jnp.cos(phase), -jnp.sin(phase)], axis=1) * factor
    doubled = jnp.where(wavenum == 0, 1.0, 2.0).astype(F32)
    synthesis = (
        jnp.concatenate([jnp.cos(phase) * doubled, -jnp.sin(phase) * doubled], axis=1) * factor
    )
    return (analysis, synthesis)


def mm(a, b):
    return jnp.dot(a, b, preferred_element_type=F32)


def mm_nt(a, b):
    return lax.dot_general(a, b, (((1,), (1,)), ((), ())), preferred_element_type=F32)


def mm_tn(a, b):
    return lax.dot_general(a, b, (((0,), (0,)), ((), ())), preferred_element_type=F32)


def gelu_pair(x):
    c = math.sqrt(2.0 / math.pi)
    a = 0.044715
    x2 = x * x
    s = 0.5 * jnp.tanh(x * (x2 * (c * a) + c)) + 0.5
    g = x * s
    slope = s + (g - g * s) * (x2 * (6.0 * c * a) + 2.0 * c)
    return g, slope


def spectra_kernel(u_ref, ana_ref, t_ref):
    for i in range(u_ref.shape[0]):
        t_ref[i] = mm(u_ref[i], ana_ref[...]).T


def split_lanes(even, odd):
    half = even.shape[-1] // 2
    first = lax.broadcasted_iota(jnp.int32, even.shape, 1) < half
    low = jnp.where(first, even, pltpu.roll(odd, half, 1))
    high = jnp.where(first, pltpu.roll(even, half, 1), odd)
    return low, high


def mode_rows(ref, k, pairs):
    stride = 2 * MODES
    re = ref[pl.ds(k, pairs, stride=stride), :]
    im = ref[pl.ds(MODES + k, pairs, stride=stride), :]
    return jnp.concatenate(split_lanes(re, im), axis=0)


def put_mode_rows(ref, k, pairs, rows):
    stride = 2 * MODES
    re, im = split_lanes(rows[:pairs], rows[pairs:])
    ref[pl.ds(k, pairs, stride=stride), :] = re
    ref[pl.ds(MODES + k, pairs, stride=stride), :] = im


def mixer_of(upper):
    half = upper.shape[-1] // 2
    sign = jnp.where(lax.broadcasted_iota(jnp.int32, upper.shape, 1) < half, -1.0, 1.0)
    return jnp.concatenate([upper, pltpu.roll(upper, half, 1) * sign], axis=0).astype(BF16)


def main_kernel(
    t_ref, w_ref, u_ref, g_ref, skip_t_ref, up_t_ref, up_ref, down_t_ref, down_ref, syn_ref,
    res_ref, pg_ref, pay_ref, b_ref,
    m_ref, c_ref, gu_ref, gd_ref, gs_ref,
):
    q = pl.program_id(0)
    pairs = pl.num_programs(0)
    n_pairs = t_ref.shape[0] // (2 * MODES)
    length_x = u_ref.shape[-1]
    ch = up_ref.shape[0]

    @pl.when(q == 0)
    def _():
        gu_ref[...] = jnp.zeros_like(gu_ref)
        gd_ref[...] = jnp.zeros_like(gd_ref)
        gs_ref[...] = jnp.zeros_like(gs_ref)

        @pl.loop(0, MODES)
        def _(k):
            rows = mode_rows(t_ref, k, n_pairs).astype(BF16)
            put_mode_rows(m_ref, k, n_pairs, mm(rows, mixer_of(w_ref[k])))

    base = pl.multiple_of(q * (2 * MODES), 2 * MODES)
    mixed_t = m_ref[pl.ds(base, 2 * MODES), :].T.astype(BF16)
    lhs_pre = jnp.concatenate([skip_t_ref[...], mixed_t], axis=1)
    up_t, up, down_t, down = up_t_ref[...], up_ref[...], down_t_ref[...], down_ref[...]

    acc = jnp.zeros((2 * ch + 2 * MODES, 2 * ch), F32)
    gu = gu_ref[...]
    gd = gd_ref[...]
    for j in range(length_x // CHUNK):
        at = slice(j * CHUNK, (j + 1) * CHUNK)
        u = u_ref[0, :, at]
        g = g_ref[0, :, at]
        ut = jnp.concatenate([u, syn_ref[:, at]], axis=0)
        act, slope = gelu_pair(mm(lhs_pre, ut))
        act = act.astype(BF16)
        outs, grads = [], []
        for b in range(2):
            rows = slice(b * ch, (b + 1) * ch)
            hidden, hslope = gelu_pair(mm(up_t, act[rows]))
            hidden = hidden.astype(BF16)
            hgrad = (mm(down, g[rows]) * hslope).astype(BF16)
            outs.append(mm(down_t, hidden))
            gd += mm_nt(g[rows], hidden)
            grads.append(mm(up, hgrad))
            gu += mm_nt(act[rows], hgrad)
        res_ref[0, :, at] = jnp.concatenate(outs, axis=0).astype(BF16)
        pg = (jnp.concatenate(grads, axis=0) * slope).astype(BF16)
        pg_ref[0, :, at] = pg
        acc += mm_nt(ut, pg)
    gu_ref[...] = gu
    gd_ref[...] = gd
    gs_ref[...] += acc[: 2 * ch]
    c_ref[pl.ds(base, 2 * MODES), :] = acc[2 * ch :]

    @pl.when(q == pairs - 1)
    def _():
        owners = pay_ref.shape[0]
        kept = MODES // owners
        half = jnp.where(lax.broadcasted_iota(jnp.int32, (ch, 2 * ch), 1) < ch, 1.0, -1.0)

        @pl.loop(0, MODES)
        def _(k):
            spec = mode_rows(t_ref, k, n_pairs).astype(BF16)
            coef = mode_rows(c_ref, k, n_pairs).astype(BF16)
            put_mode_rows(b_ref, k, n_pairs, mm_nt(coef, mixer_of(w_ref[k])))
            moment = mm_tn(spec, coef)
            grad = moment[:ch] + pltpu.roll(moment[ch:], ch, 1) * half
            pay_ref[k // kept, pl.ds(pl.multiple_of((k % kept) * ch, ch), ch), :] = grad

        at = kept * ch
        part = ch // (owners // 2)
        skip = gs_ref[:ch] + pltpu.roll(gs_ref[ch:], ch, 1)
        small = ch // owners
        for o in range(owners):
            side, row = divmod(o, owners // 2)
            lanes = slice(side * 2 * ch, (side + 1) * 2 * ch)
            rows = slice(row * part, (row + 1) * part)
            pay_ref[o, at : at + part, :] = gu_ref[rows, lanes]
            pay_ref[o, at + part : at + 2 * part, :] = gd_ref[rows, lanes]
            pay_ref[o, at + 2 * part : at + 2 * part + small, :] = skip[o * small : (o + 1) * small]
            pay_ref[o, at + 2 * part + small :, :] = jnp.zeros((8 - small, 2 * ch), F32)


def final_kernel(pg_ref, b_ref, skip_ref, ana_ref, out_ref):
    back_t = b_ref[...].T.astype(BF16)
    lhs = jnp.concatenate([skip_ref[...], back_t], axis=1)
    rhs = jnp.concatenate([pg_ref[0], ana_ref[...]], axis=0)
    out_ref[0] = mm(lhs, rhs).astype(BF16)


def twice(weight):
    zeros = jnp.zeros_like(weight)
    upper = jnp.concatenate([weight, zeros], axis=1)
    lower = jnp.concatenate([zeros, weight], axis=1)
    return jnp.concatenate([upper, lower], axis=0)


def whole(shape):
    return pl.BlockSpec(shape, lambda *_: (0,) * len(shape))


def local(fields, spec_weight, skip_weight, up_weight, down_weight, cotangent):
    length_x, count_y, count_z, ch = fields.shape
    hid = up_weight.shape[1]
    pencils = count_y * count_z
    pairs = pencils // 2
    owners = lax.axis_size("gz")
    kept = MODES // owners
    analysis, synthesis = fourier_tables(length_x, MODES)
    analysis = analysis.astype(BF16)
    ana_t = analysis.T
    syn_t = synthesis.astype(BF16).T
    u = fields.transpose(1, 2, 3, 0).reshape(pairs, 2 * ch, length_x)
    g = cotangent.transpose(1, 2, 3, 0).reshape(pairs, 2 * ch, length_x)

    upper = jnp.concatenate([spec_weight[:, 0], spec_weight[:, 1]], axis=2)
    upper = upper.reshape(kept * ch, 2 * ch)
    gathered = sent_to_all(upper, "gz").reshape(MODES, ch, 2 * ch)

    step = 4
    big = lambda n: pl.BlockSpec((n, 2 * ch, length_x), lambda i: (i, 0, 0))
    spectra = pl.pallas_call(
        spectra_kernel,
        grid=(pairs // step,),
        in_specs=[big(step), whole((length_x, 2 * MODES))],
        out_specs=pl.BlockSpec((step, 2 * MODES, 2 * ch), lambda i: (i, 0, 0)),
        out_shape=jax.ShapeDtypeStruct((pairs, 2 * MODES, 2 * ch), F32),
        name="spectra",
    )(u, analysis).reshape(pairs * 2 * MODES, 2 * ch)

    rows = pairs * 2 * MODES
    wide = kept * ch + 2 * (2 * ch // owners) + 8
    result, pre_grad, payload, back = pl.pallas_call(
        main_kernel,
        grid=(pairs,),
        in_specs=[
            whole((rows, 2 * ch)),
            whole((MODES, ch, 2 * ch)),
            big(1),
            big(1),
            whole((2 * ch, 2 * ch)),
            whole((hid, ch)),
            whole((ch, hid)),
            whole((ch, hid)),
            whole((hid, ch)),
            whole((2 * MODES, length_x)),
        ],
        out_specs=[big(1), big(1), whole((owners, wide, 2 * ch)), whole((rows, 2 * ch))],
        out_shape=[
            jax.ShapeDtypeStruct((pairs, 2 * ch, length_x), BF16),
            jax.ShapeDtypeStruct((pairs, 2 * ch, length_x), BF16),
            jax.ShapeDtypeStruct((owners, wide, 2 * ch), F32),
            jax.ShapeDtypeStruct((rows, 2 * ch), F32),
        ],
        scratch_shapes=[
            pltpu.VMEM((rows, 2 * ch), F32),
            pltpu.VMEM((rows, 2 * ch), F32),
            pltpu.VMEM((ch, hid), F32),
            pltpu.VMEM((ch, hid), F32),
            pltpu.VMEM((2 * ch, 2 * ch), F32),
        ],
        name="main",
    )(
        spectra, gathered, u, g, twice(skip_weight.T), up_weight.T, up_weight, down_weight.T,
        down_weight, syn_t,
    )

    summed = lax.all_to_all(payload, "gz", 0, 0, tiled=True)
    grad_fields = pl.pallas_call(
        final_kernel,
        grid=(pairs,),
        in_specs=[
            big(1),
            pl.BlockSpec((2 * MODES, 2 * ch), lambda i: (i, 0)),
            whole((2 * ch, 2 * ch)),
            whole((2 * MODES, length_x)),
        ],
        out_specs=big(1),
        out_shape=jax.ShapeDtypeStruct((pairs, 2 * ch, length_x), BF16),
        name="final",
    )(pre_grad, back, twice(skip_weight), ana_t)

    total = sent_to_all(jnp.sum(summed, axis=0), "gy").sum(axis=0)
    all_pencils = pencils * lax.axis_size("gy") * owners
    cell_scale = 1.0 / math.sqrt(length_x * all_pencils)
    pencil_scale = 1.0 / math.sqrt(all_pencils)
    at = kept * ch
    part = 2 * ch // owners
    mine = total[:at].reshape(kept, ch, 2, ch).transpose(0, 2, 1, 3) * pencil_scale
    small = sent_to_all(total[at:] * cell_scale, "gz")

    def joined(block):
        return block.reshape(2, ch, 2 * ch).transpose(1, 0, 2).reshape(ch, hid)

    grad_up = joined(small[:, :part])
    grad_down = joined(small[:, part : 2 * part]).T
    grad_skip = small[:, 2 * part : 2 * part + ch // owners, :ch].reshape(ch, ch)

    def unpacked(x):
        return x.reshape(count_y, count_z, ch, length_x).transpose(3, 0, 1, 2)

    return (unpacked(result), unpacked(grad_fields), mine, grad_skip, grad_up, grad_down)


def solution(mesh):
    big = P(None, "gy", "gz", None)
    modes = P("gz", None, None, None)
    return jax.shard_map(
        local,
        mesh=mesh,
        in_specs=(big, modes, P(), P(), P(), big),
        out_specs=(big, big, modes, P(), P(), P()),
        check_vma=False,
    )
```

profile of v0, /device:TPU:1, one launch (start us, length us, event | category | flops | bytes accessed | tf_op | source)
XLA Modules:
  0.0 166.9 jit_solution(7349601563277019490)
XLA Ops:
  0.6 0.9 fusion.17
  1.5 0.1 maximum_bitcast_fusion
  1.6 1.1 broadcast_in_dim.30
  2.7 6.8 %all-to-all-start = ((f32[16,128,128]{2,1,0:T(8,128)}), f32[16,128,128]{2,1,0:T(8,128)S(1)}, u32[]{:S(2)}, u32[]{:S(2)}) async-start(f32[16,128,128]{2,1,0:T(8,128)} %broadcast_in_dim.30), calls=%async_computation | async-start | bytes 2097152 | tf_op jit(solution)/shard_map/all_to_all | solution.py:19
  9.5 0.8 copy.29
  10.3 1.5 copy.30
  11.8 1.5 copy.31.down_ref
  13.3 0.5 sine_negate_fusion
  13.9 0.8 copy.28.ana_ref
  14.7 4.8 %spectra.1 = f32[16,64,128]{2,1,0:T(8,128)} custom-call(bf16[16,128,1024]{2,1,0:T(8,128)(2,1)} %bitcast.44, bf16[1024,64]{1,0:T(8,128)(2,1)} %copy.28.ana_ref), custom_call_target="tpu_custom_call" | custom-call | tf_op jit(solution)/shard_map/spectra/pallas_call | solution.py:215
  19.5 0.7 fusion.14.skip_t_ref
  20.2 0.5 broadcast_multiply_fusion.1
  20.8 0.7 fusion.5.syn_ref
  21.4 3.8 %all-to-all-done = f32[16,128,128]{2,1,0:T(8,128)S(1)} async-done(((f32[16,128,128]{2,1,0:T(8,128)}), f32[16,128,128]{2,1,0:T(8,128)S(1)}, u32[]{:S(2)}, u32[]{:S(2)}) %all-to-all-start) | async-done | bytes 1048608 | tf_op jit(solution)/shard_map/all_to_all | solution.py:19
  25.3 1.0 copy-done
  26.2 83.3 %main.1 = (bf16[16,128,1024]{2,1,0:T(8,128)(2,1)}, bf16[16,128,1024]{2,1,0:T(8,128)(2,1)}, f32[16,152,128]{2,1,0:T(8,128)}, f32[1024,128]{1,0:T(8,128)}) custom-call(f32[1024,128]{1,0:T(8,128)} %bitcast.49, f32[32,64,128]{2,1,0:T(8,128)} %bitcast.46, bf16[16,128,1024]{2,1,0:T(8,128)(2,1)} %bitcast.45, bf16[16,128,1024]{2,1,0:T(8,128)(2,1)} %bitcast.47, ...), custom_call_target="tpu_custom_call" | custom-call | tf_op jit(solution)/shard_map/main/pallas_call | solution.py:226
  109.5 0.0 copy-start.1
  109.6 22.2 %all_to_all.20 = f32[16,152,128]{2,1,0:T(8,128)S(1)} all-to-all(f32[16,152,128]{2,1,0:T(8,128)} %get-tuple-element.13), channel_id=1, replica_groups=mesh['gy'=8,'gz'=16] {'gz'}, dimensions={0} | all-to-all | bytes 2490368 | tf_op jit(solution)/shard_map/all_to_all | solution.py:261
  131.8 0.1 reduce_sum.18
  131.8 0.9 broadcast_in_dim.33
  132.7 7.4 %all-to-all-start.2 = ((f32[8,152,128]{2,1,0:T(8,128)}), f32[8,152,128]{2,1,0:T(8,128)S(1)}, u32[]{:S(2)}, u32[]{:S(2)}) async-start(f32[8,152,128]{2,1,0:T(8,128)} %broadcast_in_dim.33), calls=%async_computation.2 | async-start | bytes 1245184 | tf_op jit(solution)/shard_map/all_to_all | solution.py:19
  140.1 0.7 fusion.15.skip_ref
  140.8 0.7 fusion.18.ana_ref
  141.4 12.0 %final.1 = bf16[16,128,1024]{2,1,0:T(8,128)(2,1)} custom-call(bf16[16,128,1024]{2,1,0:T(8,128)(2,1)} %get-tuple-element.11.pg_ref, f32[1024,128]{1,0:T(8,128)} %get-tuple-element.12.b_ref, bf16[128,128]{1,0:T(8,128)(2,1)} %fusion.15.skip_ref, bf16[64,1024]{1,0:T(8,128)(2,1)} %fusion.18.ana_ref), custom_call_target="tpu_custom_call" | custom-call | tf_op jit(solution)/shard_map/final/pallas_call | solution.py:262
  153.5 0.7 broadcast_in_dim.34
  154.2 4.1 %all-to-all-start.3 = ((f32[16,24,128]{2,1,0:T(8,128)}), f32[16,24,128]{2,1,0:T(8,128)S(1)}, u32[]{:S(2)}, u32[]{:S(2)}) async-start(f32[16,24,128]{2,1,0:T(8,128)} %broadcast_in_dim.34), calls=%async_computation.3 | async-start | bytes 393216 | tf_op jit(solution)/shard_map/all_to_all | solution.py:19
  158.3 0.1 mul.95
  158.5 0.7 copy.34
  159.1 5.9 %all-to-all-done.3 = f32[16,24,128]{2,1,0:T(8,128)S(1)} async-done(((f32[16,24,128]{2,1,0:T(8,128)}), f32[16,24,128]{2,1,0:T(8,128)S(1)}, u32[]{:S(2)}, u32[]{:S(2)}) %all-to-all-start.3) | async-done | bytes 196640 | tf_op jit(solution)/shard_map/all_to_all | solution.py:19
  165.0 0.6 copy.39
  165.7 0.6 copy.40
  166.3 0.6 slice.30
  (9 shorter events, 0.1 us)
Async XLA Ops:
  2.7 22.6 %all-to-all-start = ((f32[16,128,128]{2,1,0:T(8,128)}), f32[16,128,128]{2,1,0:T(8,128)S(1)}, u32[]{:S(2)}, u32[]{:S(2)}) async-start(f32[16,128,128]{2,1,0:T(8,128)} %broadcast_in_dim.30), calls=%async_computation | async-start | bytes 2097152 | tf_op jit(solution)/shard_map/all_to_all | solution.py:19
  25.3 1.0 copy-start
  109.5 30.5 %copy-start.1 = (bf16[64,64]{1,0:T(8,128)(2,1)S(1)}, bf16[64,64]{1,0:T(8,128)(2,1)}, u32[]{:S(2)}) copy-start(bf16[64,64]{1,0:T(8,128)(2,1)} %param.8) | copy-start | bytes 24580
  132.7 20.8 %all-to-all-start.2 = ((f32[8,152,128]{2,1,0:T(8,128)}), f32[8,152,128]{2,1,0:T(8,128)S(1)}, u32[]{:S(2)}, u32[]{:S(2)}) async-start(f32[8,152,128]{2,1,0:T(8,128)} %broadcast_in_dim.33), calls=%async_computation.2 | async-start | bytes 1245184 | tf_op jit(solution)/shard_map/all_to_all | solution.py:19
  154.2 10.8 %all-to-all-start.3 = ((f32[16,24,128]{2,1,0:T(8,128)}), f32[16,24,128]{2,1,0:T(8,128)S(1)}, u32[]{:S(2)}, u32[]{:S(2)}) async-start(f32[16,24,128]{2,1,0:T(8,128)} %broadcast_in_dim.34), calls=%async_computation.3 | async-start | bytes 393216 | tf_op jit(solution)/shard_map/all_to_all | solution.py:19
where the time goes:
time: 168 us; the launch traced here: 167 us
  Pallas kernels  100 us (60%)
  blocking collectives  22.2 us (13%)
  starting transfers between devices  18.3 us (11%)
  local copies, waits for them, and re-layouts  11.8 us (7%)
  waiting for transfers between devices  9.72 us (6%)
  other arithmetic  4.03 us (2%)
    pallas_call x1, Pallas kernels, local(): pl.pallas_call(main_kernel, grid=(pairs,), in_specs=[whole((rows, 2 * ch)...  83.3 us
    all_to_all x1, blocking collectives, local(): summed = lax.all_to_all(payload, 'gz', 0, 0, tiled=True)  22.2 us
    all_to_all x3, starting transfers between devices, sent_to_all(): lax.all_to_all(jnp.broadcast_to(shard[None], (peers, *shard.shape)), axis...  18.3 us
    pallas_call x1, Pallas kernels, local(): pl.pallas_call(final_kernel, grid=(pairs,), in_specs=[big(1), pl.BlockSpe...  12 us
    all_to_all x3, waiting for transfers between devices, sent_to_all(): lax.all_to_all(jnp.broadcast_to(shard[None], (peers, *shard.shape)), axis...  9.72 us
    unnamed x8, local copies, waits for them, and re-layouts  5.43 us
    pallas_call x1, Pallas kernels, local(): pl.pallas_call(spectra_kernel, grid=(pairs // step,), in_specs=[big(step)...  4.81 us
  transfers between devices with their start and end apart: 3, of which 2 were waited for; matrix products, arithmetic and copies ran while one was open for 6% of the time, Pallas kernels for 10%

commit v1 on v0

v1 whole, which is shorter than its diff:
```python
import math

import jax
import jax.numpy as jnp
import numpy as np
from jax import lax
from jax.experimental import pallas as pl
from jax.experimental.pallas import tpu as pltpu
from jax.sharding import PartitionSpec as P

MODES = 32
BF16 = jnp.bfloat16
F32 = jnp.float32
CHUNK = 256
PER_STEP = 2
FINAL_STEP = 4
PRE_STEP = 2
SKEW = 2
UNROLL = 2


def to_group(block, axis, groups):
    peers = len(groups[0])
    return lax.all_to_all(
        jnp.broadcast_to(block[None], (peers, *block.shape)),
        axis, 0, 0, axis_index_groups=groups, tiled=True,
    )


def swapped(block, axis, mask):
    return lax.ppermute(block, axis, [(i, i ^ mask) for i in range(lax.axis_size(axis))])


def fourier_tables(length_x, kept):
    phase = np.outer(np.arange(length_x), np.arange(kept)) % length_x * (2.0 * np.pi / length_x)
    table = np.concatenate([np.cos(phase), -np.sin(phase)], axis=1) / math.sqrt(length_x)
    doubled = np.where(np.arange(2 * kept) % kept == 0, 1.0, 2.0)
    return table.astype(BF16), (table * doubled).astype(BF16)


def mm(a, b):
    return jnp.dot(a, b, preferred_element_type=F32)


def mm_nt(a, b):
    return lax.dot_general(a, b, (((1,), (1,)), ((), ())), preferred_element_type=F32)


def mm_tn(a, b):
    return lax.dot_general(a, b, (((0,), (0,)), ((), ())), preferred_element_type=F32)


def high_low(x):
    high = x.astype(BF16)
    return high, (x - high.astype(F32)).astype(BF16)


def gelu_pair(y):
    c = math.sqrt(2.0 / math.pi)
    a = 0.044715
    k = lambda v: jnp.asarray(v, y.dtype)
    y2 = y * y
    t = jnp.tanh(y * (y2 * k(8.0 * c * a) + k(2.0 * c)))
    top = t + k(1.0)
    g = y * top
    slope = top + (g - g * t) * (y2 * k(24.0 * c * a) + k(2.0 * c))
    return g, slope


def split_lanes(even, odd):
    half = even.shape[-1] // 2
    first = lax.broadcasted_iota(jnp.int32, even.shape, 1) < half
    low = jnp.where(first, even, pltpu.roll(odd, half, 1))
    high = jnp.where(first, pltpu.roll(even, half, 1), odd)
    return low, high


def mode_rows(ref, k, pairs):
    stride = 2 * MODES
    re = ref[pl.ds(k, pairs, stride=stride), :]
    im = ref[pl.ds(MODES + k, pairs, stride=stride), :]
    return jnp.concatenate(split_lanes(re, im), axis=0)


def put_mode_rows(ref, k, pairs, rows):
    stride = 2 * MODES
    re, im = split_lanes(rows[:pairs], rows[pairs:])
    ref[pl.ds(k, pairs, stride=stride), :] = re
    ref[pl.ds(MODES + k, pairs, stride=stride), :] = im


def mixer_of(upper):
    half = upper.shape[-1] // 2
    sign = jnp.where(lax.broadcasted_iota(jnp.int32, upper.shape, 1) < half, -1.0, 1.0)
    return jnp.concatenate([upper, pltpu.roll(upper, half, 1) * sign], axis=0)


def each_mode(core, mine_ref, other_ref, ch, visit):
    kept = mine_ref.shape[1] // ch

    @pl.loop(0, mine_ref.shape[0], unroll=UNROLL)
    def _(chip):
        for side, ref in enumerate((mine_ref, other_ref)):
            for i in range(kept):
                visit((chip * 2 + (core ^ side)) * kept + i, ref[chip, i * ch : (i + 1) * ch, :])


def pre_kernel(u_ref, g_ref, ana_ref, down_ref, t_ref, hc_ref):
    ch = down_ref.shape[1]
    hid = down_ref.shape[0]
    for i in range(u_ref.shape[0]):
        t_ref[i] = mm(u_ref[i], ana_ref[...]).T
        for b in range(2):
            hc_ref[i, b * hid : (b + 1) * hid] = mm(
                down_ref[...], g_ref[i, b * ch : (b + 1) * ch]
            ).astype(BF16)


def main_kernel(
    core_ref, t_ref, mine_ref, other_ref, u_ref, g_ref, hc_ref, skip_t_ref, up_t_ref, up_ref,
    down_t_ref, syn_ref,
    res_ref, pg_ref, pay_ref, c_ref,
    m_ref, gu_ref, gd_ref, gs_ref,
):
    q = pl.program_id(0)
    steps = pl.num_programs(0)
    n_pairs = t_ref.shape[0] // (2 * MODES)
    per_step = u_ref.shape[0]
    length_x = u_ref.shape[-1]
    ch, hid = up_ref.shape

    @pl.when(q == 0)
    def _():
        gu_ref[...] = jnp.zeros_like(gu_ref)
        gd_ref[...] = jnp.zeros_like(gd_ref)
        gs_ref[...] = jnp.zeros_like(gs_ref)

        def visit(k, upper):
            rows, rows_low = high_low(mode_rows(t_ref, k, n_pairs))
            mixer, mixer_low = high_low(mixer_of(upper))
            mixed = mm(
                jnp.concatenate([rows, rows_low], axis=1), jnp.concatenate([mixer, mixer], axis=0)
            )
            put_mode_rows(m_ref, k, n_pairs, mixed + mm(rows, mixer_low))

        each_mode(core_ref[0], mine_ref, other_ref, ch, visit)

    up_t, up, down_t = up_t_ref[...], up_ref[...], down_t_ref[...]
    chunks = length_x // CHUNK
    n = per_step * chunks * 2
    span = lambda j: slice(j % chunks * CHUNK, (j % chunks + 1) * CHUNK)
    lane = lambda b: slice(b * ch, (b + 1) * ch)
    unit = lambda b: slice(b * hid, (b + 1) * hid)
    lhs_pre, pre, acts, hps, hids, outs, grads, accs = {}, {}, {}, {}, {}, {}, {}, {}
    total = {}

    def add(where, key, value):
        where[key] = where[key] + value if key in where else value

    def base(p):
        return pl.multiple_of((q * per_step + p) * (2 * MODES), 2 * MODES)

    def table_rows(j):
        return jnp.concatenate([u_ref[j // chunks, :, span(j)], syn_ref[:, span(j)]], axis=0)

    def first(j):
        p = j // chunks
        if j % chunks == 0:
            mixed, mixed_low = high_low(m_ref[pl.ds(base(p), 2 * MODES), :].T * 0.5)
            lhs_pre[p] = jnp.concatenate([skip_t_ref[...], mixed, mixed_low], axis=1)
        rhs = jnp.concatenate([table_rows(j), syn_ref[:, span(j)]], axis=0)
        pre[j] = mm(lhs_pre[p], rhs)

    def gelu_act(j):
        act, slope = gelu_pair(pre.pop(j))
        acts[j] = (act.astype(BF16), slope)

    def widen(i):
        j, b = divmod(i, 2)
        hps[i] = mm(up_t, acts[j][0][lane(b)]).astype(BF16)

    def gelu_hidden(i):
        j, b = divmod(i, 2)
        hidden, slope = gelu_pair(hps.pop(i))
        hids[i] = (hidden, hc_ref[j // chunks, unit(b), span(j)] * slope)

    def narrow(i):
        j, b = divmod(i, 2)
        hidden, hgrad = hids.pop(i)
        outs[i] = mm(down_t, hidden)
        grads[i] = mm(up, hgrad)
        add(total, "gd", mm_nt(g_ref[j // chunks, lane(b), span(j)], hidden))
        add(total, "gu", mm_nt(acts[j][0][lane(b)], hgrad))

    def last(j):
        p = j // chunks
        out = jnp.concatenate([outs.pop(2 * j), outs.pop(2 * j + 1)], axis=0)
        res_ref[p, :, span(j)] = out.astype(BF16)
        both = jnp.concatenate([grads.pop(2 * j), grads.pop(2 * j + 1)], axis=0)
        pg = (both * acts.pop(j)[1]).astype(BF16)
        pg_ref[p, :, span(j)] = pg
        add(accs, p, mm_nt(table_rows(j), pg))
        if j % chunks == chunks - 1:
            acc = accs.pop(p)
            add(total, "gs", acc[: 2 * ch])
            c_ref[pl.ds(base(p), 2 * MODES), :] = acc[2 * ch :]

    ahead = SKEW * 2
    for i in range(-ahead, n + 2):
        j, b = divmod(i + ahead, 2)
        if b == 0 and 0 <= j < n // 2:
            first(j)
            gelu_act(j)
        if 0 <= i + 1 < n:
            widen(i + 1)
        if 0 <= i < n:
            gelu_hidden(i)
        if 0 <= i - 1 < n:
            narrow(i - 1)
            if (i - 1) % 2 == 1:
                last((i - 1) // 2)
    gu_ref[...] += total["gu"]
    gd_ref[...] += total["gd"]
    gs_ref[...] += total["gs"]

    @pl.when(q == steps - 1)
    def _():
        chips = pay_ref.shape[1]
        kept = MODES // (2 * chips)
        sign = jnp.where(lax.broadcasted_iota(jnp.int32, (ch, 2 * ch), 1) < ch, 1.0, -1.0)

        @pl.loop(0, chips, unroll=UNROLL)
        def _(chip):
            for core in range(2):
                for i in range(kept):
                    k = (chip * 2 + core) * kept + i
                    spec = mode_rows(t_ref, k, n_pairs).astype(BF16)
                    coef = mode_rows(c_ref, k, n_pairs).astype(BF16)
                    moment = mm_tn(spec, coef)
                    grad = moment[:ch] + pltpu.roll(moment[ch:], ch, 1) * sign
                    pay_ref[core, chip, i * ch : (i + 1) * ch, :] = grad

        at = kept * ch
        part = ch // chips
        skip = gs_ref[:ch] + pltpu.roll(gs_ref[ch:], ch, 1)
        small = ch // (2 * chips)
        for o in range(2 * chips):
            chip, core = divmod(o, 2)
            side, row = divmod(o, chips)
            lanes = slice(side * 2 * ch, (side + 1) * 2 * ch)
            rows = slice(row * part, (row + 1) * part)
            pay_ref[core, chip, at : at + part, :] = gu_ref[rows, lanes]
            pay_ref[core, chip, at + part : at + 2 * part, :] = gd_ref[rows, lanes]
            tail = jnp.concatenate(
                [skip[o * small : (o + 1) * small], jnp.zeros((8 - small, 2 * ch), F32)], axis=0
            )
            pay_ref[core, chip, at + 2 * part : at + 2 * part + 8, :] = tail


def final_kernel(core_ref, c_ref, mine_ref, other_ref, pg_ref, skip_ref, ana_ref, out_ref, b_ref):
    q = pl.program_id(0)
    n_pairs = c_ref.shape[0] // (2 * MODES)
    per_step = pg_ref.shape[0]

    @pl.when(q == 0)
    def _():
        def visit(k, upper):
            coef = mode_rows(c_ref, k, n_pairs).astype(BF16)
            put_mode_rows(b_ref, k, n_pairs, mm_nt(coef, mixer_of(upper).astype(BF16)))

        each_mode(core_ref[0], mine_ref, other_ref, skip_ref.shape[0] // 2, visit)

    for p in range(per_step):
        base = pl.multiple_of((q * per_step + p) * (2 * MODES), 2 * MODES)
        back, back_low = high_low(b_ref[pl.ds(base, 2 * MODES), :].T)
        lhs = jnp.concatenate([skip_ref[...], back, back_low], axis=1)
        rhs = jnp.concatenate([pg_ref[p], ana_ref[...], ana_ref[...]], axis=0)
        out_ref[p] = mm(lhs, rhs).astype(BF16)


def twice(weight):
    zeros = jnp.zeros_like(weight)
    upper = jnp.concatenate([weight, zeros], axis=1)
    lower = jnp.concatenate([zeros, weight], axis=1)
    return jnp.concatenate([upper, lower], axis=0)


def whole(shape):
    return pl.BlockSpec(shape, lambda *_: (0,) * len(shape))


def local(fields, spec_weight, skip_weight, up_weight, down_weight, cotangent):
    length_x, count_y, count_z, ch = fields.shape
    hid = up_weight.shape[1]
    pencils = count_y * count_z
    pairs = pencils // 2
    owners = lax.axis_size("gz")
    rows_y = lax.axis_size("gy")
    chips = owners // 2
    kept = MODES // owners
    analysis, synthesis = fourier_tables(length_x, MODES)
    u = fields.transpose(1, 2, 3, 0).reshape(pairs, 2 * ch, length_x)
    g = cotangent.transpose(1, 2, 3, 0).reshape(pairs, 2 * ch, length_x)
    core = lax.axis_index("gz") % 2
    core_word = jnp.full((1,), core, jnp.int32)
    same_core = [[i for i in range(owners) if i % 2 == c] for c in range(2)]
    columns = [[i for i in range(rows_y) if i % 2 == c] for c in range(2)]

    upper = jnp.concatenate([spec_weight[:, 0], spec_weight[:, 1]], axis=2)
    mine = to_group(upper.reshape(kept * ch, 2 * ch), "gz", same_core)
    other = swapped(mine, "gz", 1)

    def big(n, rows=2 * ch):
        return pl.BlockSpec((n, rows, length_x), lambda i: (i, 0, 0))

    rows = pairs * 2 * MODES
    cells = pencils * length_x
    half = BF16(0.5)
    spectra, hidden_cot = pl.pallas_call(
        pre_kernel,
        grid=(pairs // PRE_STEP,),
        in_specs=[big(PRE_STEP), big(PRE_STEP), whole((length_x, 2 * MODES)), whole((hid, ch))],
        out_specs=[
            pl.BlockSpec((PRE_STEP, 2 * MODES, 2 * ch), lambda i: (i, 0, 0)),
            big(PRE_STEP, 2 * hid),
        ],
        out_shape=[
            jax.ShapeDtypeStruct((pairs, 2 * MODES, 2 * ch), F32),
            jax.ShapeDtypeStruct((pairs, 2 * hid, length_x), BF16),
        ],
        cost_estimate=pl.CostEstimate(
            flops=2 * cells * ch * (hid + 2 * MODES), bytes_accessed=cells * 12 * ch, transcendentals=0
        ),
        name="pre",
    )(u, g, analysis, down_weight * half)
    spectra = spectra.reshape(rows, 2 * ch)

    wide = kept * ch + 2 * (2 * ch // owners) + 8
    smem = pl.BlockSpec(memory_space=pltpu.SMEM)
    weights = whole((chips, kept * ch, 2 * ch))
    result, pre_grad, payload, coeffs = pl.pallas_call(
        main_kernel,
        grid=(pairs // PER_STEP,),
        in_specs=[
            smem,
            whole((rows, 2 * ch)),
            weights,
            weights,
            big(PER_STEP),
            big(PER_STEP),
            big(PER_STEP, 2 * hid),
            whole((2 * ch, 2 * ch)),
            whole((hid, ch)),
            whole((ch, hid)),
            whole((ch, hid)),
            whole((2 * MODES, length_x)),
        ],
        out_specs=[big(PER_STEP), big(PER_STEP), whole((2, chips, wide, 2 * ch)), whole((rows, 2 * ch))],
        out_shape=[
            jax.ShapeDtypeStruct((pairs, 2 * ch, length_x), BF16),
            jax.ShapeDtypeStruct((pairs, 2 * ch, length_x), BF16),
            jax.ShapeDtypeStruct((2, chips, wide, 2 * ch), F32),
            jax.ShapeDtypeStruct((rows, 2 * ch), F32),
        ],
        scratch_shapes=[
            pltpu.VMEM((rows, 2 * ch), F32),
            pltpu.VMEM((ch, hid), F32),
            pltpu.VMEM((ch, hid), F32),
            pltpu.VMEM((2 * ch, 2 * ch), F32),
        ],
        cost_estimate=pl.CostEstimate(
            flops=16 * cells * ch * hid, bytes_accessed=cells * 16 * ch, transcendentals=cells * hid
        ),
        name="main",
    )(
        core_word, spectra, mine, other, u, g, hidden_cot, twice(skip_weight.T) * half,
        up_weight.T * half, up_weight * half, down_weight.T, synthesis.T,
    )

    kept_half = lax.dynamic_index_in_dim(payload, core, 0, keepdims=False)
    sent_half = lax.dynamic_index_in_dim(payload, 1 - core, 0, keepdims=False)
    chip_sum = kept_half + swapped(sent_half, "gz", 1)
    arrived = lax.all_to_all(chip_sum, "gz", 0, 0, axis_index_groups=same_core, tiled=True)

    grad_fields = pl.pallas_call(
        final_kernel,
        grid=(pairs // FINAL_STEP,),
        in_specs=[
            smem,
            whole((rows, 2 * ch)),
            weights,
            weights,
            big(FINAL_STEP),
            whole((2 * ch, 2 * ch)),
            whole((2 * MODES, length_x)),
        ],
        out_specs=big(FINAL_STEP),
        out_shape=jax.ShapeDtypeStruct((pairs, 2 * ch, length_x), BF16),
        scratch_shapes=[pltpu.VMEM((rows, 2 * ch), F32)],
        cost_estimate=pl.CostEstimate(
            flops=8 * cells * ch * ch, bytes_accessed=cells * 4 * ch, transcendentals=0
        ),
        name="final",
    )(core_word, coeffs, mine, other, pre_grad, twice(skip_weight), analysis.T)

    total = jnp.sum(arrived, axis=0)
    total = total + swapped(total, "gy", 1)
    total = jnp.sum(to_group(total, "gy", columns), axis=0)
    all_pencils = pencils * rows_y * owners
    cell_scale = 1.0 / math.sqrt(length_x * all_pencils)
    pencil_scale = 1.0 / math.sqrt(all_pencils)
    at = kept * ch
    part = 2 * ch // owners
    grad_spec = total[:at].reshape(kept, ch, 2, ch).transpose(0, 2, 1, 3) * pencil_scale
    small = to_group(total[at:] * cell_scale, "gz", [list(range(owners))])

    def joined(block):
        return block.reshape(2, ch, 2 * ch).transpose(1, 0, 2).reshape(ch, hid)

    grad_up = joined(small[:, :part])
    grad_down = joined(small[:, part : 2 * part]).T
    grad_skip = small[:, 2 * part : 2 * part + ch // owners, :ch].reshape(ch, ch)

    def unpacked(x):
        return x.reshape(count_y, count_z, ch, length_x).transpose(3, 0, 1, 2)

    return (unpacked(result), unpacked(grad_fields), grad_spec, grad_skip, grad_up, grad_down)


def solution(mesh):
    big = P(None, "gy", "gz", None)
    modes = P("gz", None, None, None)

    return jax.shard_map(
        local,
        mesh=mesh,
        in_specs=(big, modes, P(), P(), P(), big),
        out_specs=(big, big, modes, P(), P(), P()),
        check_vma=False,
    )
```

time: 168 us -> 125 us (0.74)
  Pallas kernels: 100 us -> 56.1 us
  blocking collectives: 22.2 us -> 28.3 us
  local copies, waits for them, and re-layouts: 11.8 us -> 8.75 us
  starting transfers between devices: 18.3 us -> 15.5 us
    pallas_call x3, Pallas kernels: 100 us -> 56.1 us  [the longest x1 34.9 us: local(): pl.pallas_call(main_kernel, grid=(pairs // PER_STEP,), in_specs=[smem, wh...]
    all_to_all x3 -> x2, starting transfers between devices: 18.3 us -> 10.8 us  [to_group(): lax.all_to_all(jnp.broadcast_to(block[None], (peers, *block.shape)), axis...]
    all_to_all x1 -> x2, blocking collectives: 22.2 us -> 28.3 us  [the longest x1 14.9 us: to_group(): lax.all_to_all(jnp.broadcast_to(block[None], (peers, *block.shape)), axis...]
    ppermute x0 -> x3, starting transfers between devices: none -> 4.62 us  [swapped(): lax.ppermute(block, axis, [(i, i ^ mask) for i in range(lax.axis_size(axi...]
    ppermute x0 -> x3, waiting for transfers between devices: none -> 4.15 us  [swapped(): lax.ppermute(block, axis, [(i, i ^ mask) for i in range(lax.axis_size(axi...]
    all_to_all x3 -> x2, waiting for transfers between devices: 9.72 us -> 5.89 us  [to_group(): lax.all_to_all(jnp.broadcast_to(block[None], (peers, *block.shape)), axis...]
    unnamed x8 -> x9, local copies, waits for them, and re-layouts: 5.43 us -> 3.13 us
    mul x2 -> x4, other arithmetic: 0.54 us -> 2.71 us  [the longest x1 1.38 us: local(): up_weight.T * half]
  transfers between devices with their start and end apart: 3 -> 5, of which waited for: 2 -> 3; matrix products, arithmetic and copies ran while one was open for 6% -> 5% of each run, Pallas kernels for 10% -> 17%
where the time goes in v1:
time: 125 us; the launch traced here: 124 us
  Pallas kernels  56.1 us (45%)
  blocking collectives  28.3 us (23%)
  starting transfers between devices  15.5 us (12%)
  waiting for transfers between devices  10 us (8%)
  local copies, waits for them, and re-layouts  8.75 us (7%)
  other arithmetic  4.7 us (4%)
    pallas_call x1, Pallas kernels, local(): pl.pallas_call(main_kernel, grid=(pairs // PER_STEP,), in_specs=[smem, wh...  34.9 us
    all_to_all x1, blocking collectives, to_group(): lax.all_to_all(jnp.broadcast_to(block[None], (peers, *block.shape)), axis...  14.9 us
    all_to_all x1, blocking collectives, local(): lax.all_to_all(chip_sum, 'gz', 0, 0, axis_index_groups=same_core, tiled=T...  13.4 us
    pallas_call x1, Pallas kernels, local(): pl.pallas_call(pre_kernel, grid=(pairs // PRE_STEP,), in_specs=[big(PRE_S...  13.1 us
    all_to_all x2, starting transfers between devices, to_group(): lax.all_to_all(jnp.broadcast_to(block[None], (peers, *block.shape)), axis...  10.8 us
    pallas_call x1, Pallas kernels, local(): pl.pallas_call(final_kernel, grid=(pairs // FINAL_STEP,), in_specs=[smem,...  8.09 us
    all_to_all x2, waiting for transfers between devices, to_group(): lax.all_to_all(jnp.broadcast_to(block[None], (peers, *block.shape)), axis...  5.89 us
    ppermute x3, starting transfers between devices, swapped(): lax.ppermute(block, axis, [(i, i ^ mask) for i in range(lax.axis_size(axi...  4.62 us
  transfers between devices with their start and end apart: 5, of which 3 were waited for; matrix products, arithmetic and copies ran while one was open for 5% of the time, Pallas kernels for 17%

profile of v1, /device:TPU:1, one launch (start us, length us, event | category | flops | bytes accessed | tf_op | source)
XLA Modules:
  0.0 124.1 jit_solution(3041499567677735750)
XLA Ops:
  0.6 0.9 fusion.9
  1.5 0.1 maximum_bitcast_fusion
  1.7 14.9 %all_to_all.20.mine_ref = f32[8,128,128]{2,1,0:T(8,128)S(1)} all-to-all(f32[8,128,128]{2,1,0:T(8,128)S(1)} %broadcast_in_dim.24), channel_id=1, replica_groups={{0,2,4,6,8,10,12,14},{1,3,5,7,9,11,13,15},{16,18,20,22,24,26,28,30},{17..., dimensions={0} | all-to-all | bytes 1048576 | tf_op jit(solution)/shard_map/all_to_all | solution.py:24
  16.5 1.8 %collective-permute-start = (f32[8,128,128]{2,1,0:T(8,128)S(1)}, f32[8,128,128]{2,1,0:T(8,128)S(1)}, u32[]{:S(2)}, u32[]{:S(2)}) collective-permute-start(f32[8,128,128]{2,1,0:T(8,128)S(1)} %all_to_all.20.mine_ref), channel_id=1, source_target_pairs={{0,1},{1,0},{2,3},{3,2},{4,5},{5,4},{6,7},{7,6},{8,9},{9,8},{10,11... | collective-permute-start | bytes 1572872 | tf_op jit(solution)/shard_map/ppermute | solution.py:31
  18.3 1.4 %broadcast_multiply_fusion.1 = (bf16[64,256]{1,0:T(8,128)(2,1)}, bf16[256,64]{0,1:T(8,128)(2,1)S(1)}) fusion(bf16[64,256]{1,0:T(8,128)(2,1)} %param.12), kind=kLoop, calls=%fused_computation.16 | loop fusion | flops 16384 | bytes 98304 | tf_op jit(solution)/shard_map/mul | solution.py:377
  19.7 0.9 copy.34
  20.6 0.7 copy.37.up_t_ref
  21.3 0.8 copy.36
  22.1 0.7 fusion.5.skip_t_ref
  22.8 0.6 broadcast_multiply_fusion.down_ref
  23.5 13.1 %pre.1 = (f32[16,64,128]{2,1,0:T(8,128)}, bf16[16,512,1024]{2,1,0:T(8,128)(2,1)}) custom-call(bf16[16,128,1024]{2,1,0:T(8,128)(2,1)} %bitcast.43, bf16[16,128,1024]{2,1,0:T(8,128)(2,1)} %bitcast.45, bf16[1024,64]{1,0:T(8,128)(2,1)} %constant.44.clone.ana_ref, bf16[256,64]{1,0:T(8,128)(2,1)} %broadcast_multiply_fusion.down_ref), custom_call_target="tpu_custom_call" | custom-call | flops 1342177280 | bytes 25165824 | tf_op jit(solution)/shard_map/pre/pallas_call | solution.py:319
  36.6 0.8 copy-done.1
  37.4 34.9 %main.1 = (bf16[16,128,1024]{2,1,0:T(8,128)(2,1)}, bf16[16,128,1024]{2,1,0:T(8,128)(2,1)}, f32[2,8,152,128]{3,2,1,0:T(8,128)}, f32[1024,128]{1,0:T(8,128)}) custom-call(s32[1]{0:T(128)} %bitcast.core_ref, f32[1024,128]{1,0:T(8,128)} %bitcast.55, f32[8,128,128]{2,1,0:T(8,128)} %copy-done, f32[8,128,128]{2,1,0:T(8,128)} %copy-done.1, ...), custom_call_target="tpu_custom_call" | custom-call | flops 8589934592 | bytes 33554432 | tf_op jit(solution)/shard_map/main/pallas_call | solution.py:341
  72.3 0.0 copy-start.2
  72.3 1.1 dynamic-slice_bitcast_fusion
  73.4 0.1 collective-permute-start.1
  73.5 2.0 %collective-permute-done.1 = f32[8,152,128]{2,1,0:T(8,128)S(1)} collective-permute-done((f32[8,152,128]{2,1,0:T(8,128)S(1)}, f32[8,152,128]{2,1,0:T(8,128)S(1)}, u32[]{:S(2)}, u32[]{:S(2)}) %collective-permute-start.1) | collective-permute-done | bytes 622624 | tf_op jit(solution)/shard_map/ppermute | solution.py:31
  75.5 1.1 bitcast_add_fusion
  76.7 13.4 %all_to_all.21 = f32[8,152,128]{2,1,0:T(8,128)S(1)} all-to-all(f32[8,152,128]{2,1,0:T(8,128)S(1)} %bitcast_add_fusion), channel_id=1, replica_groups={{0,2,4,6,8,10,12,14},{1,3,5,7,9,11,13,15},{16,18,20,22,24,26,28,30},{17..., dimensions={0} | all-to-all | bytes 1245184 | tf_op jit(solution)/shard_map/all_to_all | solution.py:383
  90.1 2.7 %collective-permute-start.2 = (f32[152,128]{1,0:T(8,128)S(1)}, f32[152,128]{1,0:T(8,128)S(1)}, u32[]{:S(2)}, u32[]{:S(2)}) collective-permute-start(f32[152,128]{1,0:T(8,128)S(1)} %reduce_sum.18), channel_id=1, source_target_pairs={{0,16},{16,0},{32,48},{48,32},{64,80},{80,64},{96,112},{112,96},{1... | collective-permute-start | bytes 233480 | tf_op jit(solution)/shard_map/ppermute | solution.py:31
  92.8 2.1 %collective-permute-done.2 = f32[152,128]{1,0:T(8,128)S(1)} collective-permute-done((f32[152,128]{1,0:T(8,128)S(1)}, f32[152,128]{1,0:T(8,128)S(1)}, u32[]{:S(2)}, u32[]{:S(2)}) %collective-permute-start.2) | collective-permute-done | bytes 77856 | tf_op jit(solution)/shard_map/ppermute | solution.py:31
  95.0 0.7 broadcast_in_dim.25
  95.7 5.0 %all-to-all-start.2 = ((f32[4,152,128]{2,1,0:T(8,128)}), f32[4,152,128]{2,1,0:T(8,128)S(1)}, u32[]{:S(2)}, u32[]{:S(2)}) async-start(f32[4,152,128]{2,1,0:T(8,128)} %broadcast_in_dim.25), calls=%async_computation.2 | async-start | bytes 622592 | tf_op jit(solution)/shard_map/all_to_all | solution.py:24
  100.8 0.7 fusion.6.skip_ref
  101.5 8.1 %final.1 = bf16[16,128,1024]{2,1,0:T(8,128)(2,1)} custom-call(s32[1]{0:T(128)} %bitcast.core_ref, f32[1024,128]{1,0:T(8,128)} %get-tuple-element.15.c_ref, f32[8,128,128]{2,1,0:T(8,128)} %copy-done, f32[8,128,128]{2,1,0:T(8,128)} %copy-done.1, bf16[16,128,1024]{2,1,0:T(8,128)(2,1)} %get-tuple-element.16.pg_ref, bf16[128,128]{1,0:T(8,128)(2,1)} %fusion.6.skip_ref, ...), custom_call_target="tpu_custom_call" | custom-call | flops 1073741824 | bytes 8388608 | tf_op jit(solution)/shard_map/final/pallas_call | solution.py:385
  109.6 0.7 broadcast_in_dim.26
  110.3 5.8 %all-to-all-start.3 = ((f32[16,24,128]{2,1,0:T(8,128)}), f32[16,24,128]{2,1,0:T(8,128)S(1)}, u32[]{:S(2)}, u32[]{:S(2)}) async-start(f32[16,24,128]{2,1,0:T(8,128)} %broadcast_in_dim.26), calls=%async_computation.3 | async-start | bytes 393216 | tf_op jit(solution)/shard_map/all_to_all | solution.py:24
  116.1 0.1 mul.41
  116.2 0.7 copy.40
  116.9 5.9 %all-to-all-done.3 = f32[16,24,128]{2,1,0:T(8,128)S(1)} async-done(((f32[16,24,128]{2,1,0:T(8,128)}), f32[16,24,128]{2,1,0:T(8,128)S(1)}, u32[]{:S(2)}, u32[]{:S(2)}) %all-to-all-start.3) | async-done | bytes 196640 | tf_op jit(solution)/shard_map/all_to_all | solution.py:24
  122.8 0.7 bitcast_bitcast_fusion
  123.4 0.6 slice.30
  (13 shorter events, 0.1 us)
Async XLA Ops:
  16.5 20.0 %copy-start = (f32[8,128,128]{2,1,0:T(8,128)}, f32[8,128,128]{2,1,0:T(8,128)S(1)}, u32[]{:S(2)}) copy-start(f32[8,128,128]{2,1,0:T(8,128)S(1)} %all_to_all.20.mine_ref) | copy-start | bytes 1572868
  16.5 20.1 %collective-permute-start = (f32[8,128,128]{2,1,0:T(8,128)S(1)}, f32[8,128,128]{2,1,0:T(8,128)S(1)}, u32[]{:S(2)}, u32[]{:S(2)}) collective-permute-start(f32[8,128,128]{2,1,0:T(8,128)S(1)} %all_to_all.20.mine_ref), channel_id=1, source_target_pairs={{0,1},{1,0},{2,3},{3,2},{4,5},{5,4},{6,7},{7,6},{8,9},{9,8},{10,11... | collective-permute-start | bytes 1572872 | tf_op jit(solution)/shard_map/ppermute | solution.py:31
  36.6 0.8 copy-start.1
  72.3 28.5 %copy-start.2 = (bf16[64,64]{1,0:T(8,128)(2,1)S(1)}, bf16[64,64]{1,0:T(8,128)(2,1)}, u32[]{:S(2)}) copy-start(bf16[64,64]{1,0:T(8,128)(2,1)} %param.11) | copy-start | bytes 24580
  73.4 2.1 %collective-permute-start.1 = (f32[8,152,128]{2,1,0:T(8,128)S(1)}, f32[8,152,128]{2,1,0:T(8,128)S(1)}, u32[]{:S(2)}, u32[]{:S(2)}) collective-permute-start(f32[8,152,128]{2,1,0:T(8,128)S(1)} %dynamic-slice_bitcast_fusion), channel_id=1, source_target_pairs={{0,1},{1,0},{2,3},{3,2},{4,5},{5,4},{6,7},{7,6},{8,9},{9,8},{10,11... | collective-permute-start | bytes 1867784 | tf_op jit(solution)/shard_map/ppermute | solution.py:31
  90.1 4.8 %collective-permute-start.2 = (f32[152,128]{1,0:T(8,128)S(1)}, f32[152,128]{1,0:T(8,128)S(1)}, u32[]{:S(2)}, u32[]{:S(2)}) collective-permute-start(f32[152,128]{1,0:T(8,128)S(1)} %reduce_sum.18), channel_id=1, source_target_pairs={{0,16},{16,0},{32,48},{48,32},{64,80},{80,64},{96,112},{112,96},{1... | collective-permute-start | bytes 233480 | tf_op jit(solution)/shard_map/ppermute | solution.py:31
  95.7 13.8 %all-to-all-start.2 = ((f32[4,152,128]{2,1,0:T(8,128)}), f32[4,152,128]{2,1,0:T(8,128)S(1)}, u32[]{:S(2)}, u32[]{:S(2)}) async-start(f32[4,152,128]{2,1,0:T(8,128)} %broadcast_in_dim.25), calls=%async_computation.2 | async-start | bytes 622592 | tf_op jit(solution)/shard_map/all_to_all | solution.py:24
  110.3 12.5 %all-to-all-start.3 = ((f32[16,24,128]{2,1,0:T(8,128)}), f32[16,24,128]{2,1,0:T(8,128)S(1)}, u32[]{:S(2)}, u32[]{:S(2)}) async-start(f32[16,24,128]{2,1,0:T(8,128)} %broadcast_in_dim.26), calls=%async_computation.3 | async-start | bytes 393216 | tf_op jit(solution)/shard_map/all_to_all | solution.py:24

commit v2 on v1

--- a/solution.py
+++ b/solution.py
@@ -14,7 +14,8 @@
 CHUNK = 256
 PER_STEP = 2
 FINAL_STEP = 4
-PRE_STEP = 2
+PRE_STEP = 4
+PRE_CHUNK = 1024
 SKEW = 2
 UNROLL = 2
 
@@ -105,21 +106,23 @@
                 visit((chip * 2 + (core ^ side)) * kept + i, ref[chip, i * ch : (i + 1) * ch, :])
 
 
-def pre_kernel(u_ref, g_ref, ana_ref, down_ref, t_ref, hc_ref):
-    ch = down_ref.shape[1]
-    hid = down_ref.shape[0]
+def pre_kernel(u_ref, g_ref, ana_ref, down_t_ref, t_ref, hc_ref):
+    ch, hid = down_t_ref.shape
+    length_x = u_ref.shape[-1]
+    down = down_t_ref[...].T * BF16(0.5)
     for i in range(u_ref.shape[0]):
         t_ref[i] = mm(u_ref[i], ana_ref[...]).T
-        for b in range(2):
-            hc_ref[i, b * hid : (b + 1) * hid] = mm(
-                down_ref[...], g_ref[i, b * ch : (b + 1) * ch]
-            ).astype(BF16)
+        for j in range(length_x // PRE_CHUNK):
+            span = slice(j * PRE_CHUNK, (j + 1) * PRE_CHUNK)
+            for b in range(2):
+                hc = mm(down, g_ref[i, b * ch : (b + 1) * ch, span])
+                hc_ref[i, b * hid : (b + 1) * hid, span] = hc.astype(BF16)
 
 
 def main_kernel(
     core_ref, t_ref, mine_ref, other_ref, u_ref, g_ref, hc_ref, skip_t_ref, up_t_ref, up_ref,
     down_t_ref, syn_ref,
-    res_ref, pg_ref, pay_ref, c_ref,
+    res_ref, pg_ref, kept_ref, sent_ref, c_ref,
     m_ref, gu_ref, gd_ref, gs_ref,
 ):
     q = pl.program_id(0)
@@ -225,36 +228,35 @@
 
     @pl.when(q == steps - 1)
     def _():
-        chips = pay_ref.shape[1]
+        chips = kept_ref.shape[0]
         kept = MODES // (2 * chips)
+        mine = core_ref[0]
         sign = jnp.where(lax.broadcasted_iota(jnp.int32, (ch, 2 * ch), 1) < ch, 1.0, -1.0)
 
         @pl.loop(0, chips, unroll=UNROLL)
         def _(chip):
-            for core in range(2):
+            for side, ref in enumerate((kept_ref, sent_ref)):
                 for i in range(kept):
-                    k = (chip * 2 + core) * kept + i
+                    k = (chip * 2 + (mine ^ side)) * kept + i
                     spec = mode_rows(t_ref, k, n_pairs).astype(BF16)
                     coef = mode_rows(c_ref, k, n_pairs).astype(BF16)
                     moment = mm_tn(spec, coef)
                     grad = moment[:ch] + pltpu.roll(moment[ch:], ch, 1) * sign
-                    pay_ref[core, chip, i * ch : (i + 1) * ch, :] = grad
+                    ref[chip, i * ch : (i + 1) * ch, :] = grad
 
         at = kept * ch
         part = ch // chips
-        skip = gs_ref[:ch] + pltpu.roll(gs_ref[ch:], ch, 1)
+        gs_ref[:ch] += pltpu.roll(gs_ref[ch:], ch, 1)
         small = ch // (2 * chips)
-        for o in range(2 * chips):
-            chip, core = divmod(o, 2)
-            side, row = divmod(o, chips)
-            lanes = slice(side * 2 * ch, (side + 1) * 2 * ch)
-            rows = slice(row * part, (row + 1) * part)
-            pay_ref[core, chip, at : at + part, :] = gu_ref[rows, lanes]
-            pay_ref[core, chip, at + part : at + 2 * part, :] = gd_ref[rows, lanes]
-            tail = jnp.concatenate(
-                [skip[o * small : (o + 1) * small], jnp.zeros((8 - small, 2 * ch), F32)], axis=0
-            )
-            pay_ref[core, chip, at + 2 * part : at + 2 * part + 8, :] = tail
+        for chip in range(chips):
+            half_at = slice(chip // (chips // 2) * 2 * ch, (chip // (chips // 2) + 1) * 2 * ch)
+            for side, ref in enumerate((kept_ref, sent_ref)):
+                o = chip * 2 + (mine ^ side)
+                rows = pl.ds(pl.multiple_of(o % chips * part, part), part)
+                ref[chip, at : at + part, :] = gu_ref[rows, half_at]
+                ref[chip, at + part : at + 2 * part, :] = gd_ref[rows, half_at]
+                ref[chip, at + 2 * part : at + 2 * part + 8, :] = jnp.zeros((8, 2 * ch), F32)
+                ref[chip, at + 2 * part : at + 2 * part + small, :] = gs_ref[pl.ds(o * small, small), :]
 
 
 def final_kernel(core_ref, c_ref, mine_ref, other_ref, pg_ref, skip_ref, ana_ref, out_ref, b_ref):
@@ -304,7 +306,6 @@
     core = lax.axis_index("gz") % 2
     core_word = jnp.full((1,), core, jnp.int32)
     same_core = [[i for i in range(owners) if i % 2 == c] for c in range(2)]
-    columns = [[i for i in range(rows_y) if i % 2 == c] for c in range(2)]
 
     upper = jnp.concatenate([spec_weight[:, 0], spec_weight[:, 1]], axis=2)
     mine = to_group(upper.reshape(kept * ch, 2 * ch), "gz", same_core)
@@ -319,7 +320,7 @@
     spectra, hidden_cot = pl.pallas_call(
         pre_kernel,
         grid=(pairs // PRE_STEP,),
-        in_specs=[big(PRE_STEP), big(PRE_STEP), whole((length_x, 2 * MODES)), whole((hid, ch))],
+        in_specs=[big(PRE_STEP), big(PRE_STEP), whole((length_x, 2 * MODES)), whole((ch, hid))],
         out_specs=[
             pl.BlockSpec((PRE_STEP, 2 * MODES, 2 * ch), lambda i: (i, 0, 0)),
             big(PRE_STEP, 2 * hid),
@@ -332,13 +333,13 @@
             flops=2 * cells * ch * (hid + 2 * MODES), bytes_accessed=cells * 12 * ch, transcendentals=0
         ),
         name="pre",
-    )(u, g, analysis, down_weight * half)
+    )(u, g, analysis, down_weight.T)
     spectra = spectra.reshape(rows, 2 * ch)
 
     wide = kept * ch + 2 * (2 * ch // owners) + 8
     smem = pl.BlockSpec(memory_space=pltpu.SMEM)
     weights = whole((chips, kept * ch, 2 * ch))
-    result, pre_grad, payload, coeffs = pl.pallas_call(
+    result, pre_grad, kept_half, sent_half, coeffs = pl.pallas_call(
         main_kernel,
         grid=(pairs // PER_STEP,),
         in_specs=[
@@ -355,11 +356,14 @@
             whole((ch, hid)),
             whole((2 * MODES, length_x)),
         ],
-        out_specs=[big(PER_STEP), big(PER_STEP), whole((2, chips, wide, 2 * ch)), whole((rows, 2 * ch))],
+        out_specs=[big(PER_STEP), big(PER_STEP)]
+        + [whole((chips, wide, 2 * ch))] * 2
+        + [whole((rows, 2 * ch))],
         out_shape=[
             jax.ShapeDtypeStruct((pairs, 2 * ch, length_x), BF16),
             jax.ShapeDtypeStruct((pairs, 2 * ch, length_x), BF16),
-            jax.ShapeDtypeStruct((2, chips, wide, 2 * ch), F32),
+            jax.ShapeDtypeStruct((chips, wide, 2 * ch), F32),
+            jax.ShapeDtypeStruct((chips, wide, 2 * ch), F32),
             jax.ShapeDtypeStruct((rows, 2 * ch), F32),
         ],
         scratch_shapes=[
@@ -377,8 +381,6 @@
         up_weight.T * half, up_weight * half, down_weight.T, synthesis.T,
     )
 
-    kept_half = lax.dynamic_index_in_dim(payload, core, 0, keepdims=False)
-    sent_half = lax.dynamic_index_in_dim(payload, 1 - core, 0, keepdims=False)
     chip_sum = kept_half + swapped(sent_half, "gz", 1)
     arrived = lax.all_to_all(chip_sum, "gz", 0, 0, axis_index_groups=same_core, tiled=True)
 
@@ -404,15 +406,19 @@
     )(core_word, coeffs, mine, other, pre_grad, twice(skip_weight), analysis.T)
 
     total = jnp.sum(arrived, axis=0)
-    total = total + swapped(total, "gy", 1)
-    total = jnp.sum(to_group(total, "gy", columns), axis=0)
     all_pencils = pencils * rows_y * owners
     cell_scale = 1.0 / math.sqrt(length_x * all_pencils)
     pencil_scale = 1.0 / math.sqrt(all_pencils)
     at = kept * ch
     part = 2 * ch // owners
-    grad_spec = total[:at].reshape(kept, ch, 2, ch).transpose(0, 2, 1, 3) * pencil_scale
-    small = to_group(total[at:] * cell_scale, "gz", [list(range(owners))])
+    everyone = lambda axis: [list(range(lax.axis_size(axis)))]
+    small = to_group(total[at:], "gy", everyone("gy"))
+    spec = total[:at]
+    spec = spec + swapped(spec, "gy", 1)
+    small = jnp.sum(small, axis=0) * cell_scale
+    small = to_group(small, "gz", everyone("gz"))
+    spec = (spec + swapped(spec, "gy", 2) + swapped(spec, "gy", 4) + swapped(spec, "gy", 6)) * pencil_scale
+    grad_spec = spec.reshape(kept, ch, 2, ch).transpose(0, 2, 1, 3)
 
     def joined(block):
         return block.reshape(2, ch, 2 * ch).transpose(1, 0, 2).reshape(ch, hid)

time: 125 us -> 128 us (1.024)
  blocking collectives: 28.3 us -> 14.9 us
  waiting for transfers between devices: 10 us -> 21.5 us
  starting transfers between devices: 15.5 us -> 23.2 us
  local copies, waits for them, and re-layouts: 8.75 us -> 6.7 us
  Pallas kernels: 56.1 us -> 54.8 us
    all_to_all x1 -> x0, blocking collectives: 13.4 us -> none  [local(): lax.all_to_all(chip_sum, 'gz', 0, 0, axis_index_groups=same_core, tiled=T...]
    all_to_all x0 -> x1, waiting for transfers between devices: none -> 10.5 us  [local(): lax.all_to_all(chip_sum, 'gz', 0, 0, axis_index_groups=same_core, tiled=T...]
    ppermute x3 -> x6, starting transfers between devices: 4.62 us -> 8.67 us  [swapped(): lax.ppermute(block, axis, [(i, i ^ mask) for i in range(lax.axis_size(axi...]
    all_to_all x0 -> x1, starting transfers between devices: none -> 3.54 us  [local(): lax.all_to_all(chip_sum, 'gz', 0, 0, axis_index_groups=same_core, tiled=T...]
    all_to_all x2, waiting for transfers between devices: 5.89 us -> 8.69 us  [to_group(): lax.all_to_all(jnp.broadcast_to(block[None], (peers, *block.shape)), axis...]
    ppermute x3 -> x6, waiting for transfers between devices: 4.15 us -> 2.23 us  [swapped(): lax.ppermute(block, axis, [(i, i ^ mask) for i in range(lax.axis_size(axi...]
    pallas_call x1, Pallas kernels: 13.1 us -> 11.7 us  [local(): pl.pallas_call(pre_kernel, grid=(pairs // PRE_STEP,), in_specs=[big(PRE_S...]
    unnamed x9 -> x8, local copies, waits for them, and re-layouts: 3.13 us -> 2.28 us
  transfers between devices with their start and end apart: 5 -> 9, of which waited for: 3 -> 4; matrix products, arithmetic and copies ran while one was open for 5% -> 5% of each run, Pallas kernels for 17% -> 16%
where the time goes in v2:
time: 128 us; the launch traced here: 127 us
  Pallas kernels  54.8 us (43%)
  starting transfers between devices  23.2 us (18%)
  waiting for transfers between devices  21.5 us (17%)
  blocking collectives  14.9 us (12%)
  local copies, waits for them, and re-layouts  6.7 us (5%)
  other arithmetic  4.9 us (4%)
    pallas_call x1, Pallas kernels, local(): pl.pallas_call(main_kernel, grid=(pairs // PER_STEP,), in_specs=[smem, wh...  35 us
    all_to_all x1, blocking collectives, to_group(): lax.all_to_all(jnp.broadcast_to(block[None], (peers, *block.shape)), axis...  14.9 us
    pallas_call x1, Pallas kernels, local(): pl.pallas_call(pre_kernel, grid=(pairs // PRE_STEP,), in_specs=[big(PRE_S...  11.7 us
    all_to_all x2, starting transfers between devices, to_group(): lax.all_to_all(jnp.broadcast_to(block[None], (peers, *block.shape)), axis...  11 us
    all_to_all x1, waiting for transfers between devices, local(): lax.all_to_all(chip_sum, 'gz', 0, 0, axis_index_groups=same_core, tiled=T...  10.5 us
    all_to_all x2, waiting for transfers between devices, to_group(): lax.all_to_all(jnp.broadcast_to(block[None], (peers, *block.shape)), axis...  8.69 us
    ppermute x6, starting transfers between devices, swapped(): lax.ppermute(block, axis, [(i, i ^ mask) for i in range(lax.axis_size(axi...  8.67 us
    pallas_call x1, Pallas kernels, local(): pl.pallas_call(final_kernel, grid=(pairs // FINAL_STEP,), in_specs=[smem,...  8.09 us
  transfers between devices with their start and end apart: 9, of which 4 were waited for; matrix products, arithmetic and copies ran while one was open for 5% of the time, Pallas kernels for 16%

profile of v2, /device:TPU:1, one launch (start us, length us, event | category | flops | bytes accessed | tf_op | source)
XLA Modules:
  0.0 126.7 jit_solution(17189214808964650872)
XLA Ops:
  0.6 0.9 fusion.9
  1.5 0.1 maximum_bitcast_fusion
  1.7 14.9 %all_to_all.20.mine_ref = f32[8,128,128]{2,1,0:T(8,128)S(1)} all-to-all(f32[8,128,128]{2,1,0:T(8,128)S(1)} %broadcast_in_dim.24), channel_id=1, replica_groups={{0,2,4,6,8,10,12,14},{1,3,5,7,9,11,13,15},{16,18,20,22,24,26,28,30},{17..., dimensions={0} | all-to-all | bytes 1048576 | tf_op jit(solution)/shard_map/all_to_all | solution.py:25
  16.5 1.8 %collective-permute-start = (f32[8,128,128]{2,1,0:T(8,128)S(1)}, f32[8,128,128]{2,1,0:T(8,128)S(1)}, u32[]{:S(2)}, u32[]{:S(2)}) collective-permute-start(f32[8,128,128]{2,1,0:T(8,128)S(1)} %all_to_all.20.mine_ref), channel_id=1, source_target_pairs={{0,1},{1,0},{2,3},{3,2},{4,5},{5,4},{6,7},{7,6},{8,9},{9,8},{10,11... | collective-permute-start | bytes 1572872 | tf_op jit(solution)/shard_map/ppermute | solution.py:32
  18.3 1.4 %broadcast_multiply_fusion = (bf16[64,256]{1,0:T(8,128)(2,1)}, bf16[256,64]{0,1:T(8,128)(2,1)S(1)}) fusion(bf16[64,256]{1,0:T(8,128)(2,1)} %param.12), kind=kLoop, calls=%fused_computation.13 | loop fusion | flops 16384 | bytes 98304 | tf_op jit(solution)/shard_map/mul | solution.py:381
  19.7 0.7 copy.26.up_t_ref
  20.5 0.8 copy.25
  21.3 0.7 fusion.5.skip_t_ref
  22.0 11.7 %pre.1 = (f32[16,64,128]{2,1,0:T(8,128)}, bf16[16,512,1024]{2,1,0:T(8,128)(2,1)}) custom-call(bf16[16,128,1024]{2,1,0:T(8,128)(2,1)} %bitcast.39, bf16[16,128,1024]{2,1,0:T(8,128)(2,1)} %bitcast.41, bf16[1024,64]{1,0:T(8,128)(2,1)} %constant.35.clone.ana_ref, bf16[64,256]{1,0:T(8,128)(2,1)} %bitcast.49), custom_call_target="tpu_custom_call" | custom-call | flops 1342177280 | bytes 25165824 | tf_op jit(solution)/shard_map/pre/pallas_call | solution.py:320
  33.7 0.8 copy-done.1
  34.5 35.0 %main.1 = (bf16[16,128,1024]{2,1,0:T(8,128)(2,1)}, bf16[16,128,1024]{2,1,0:T(8,128)(2,1)}, f32[8,152,128]{2,1,0:T(8,128)}, f32[8,152,128]{2,1,0:T(8,128)}, f32[1024,128]{1,0:T(8,128)}) custom-call(s32[1]{0:T(128)} %bitcast.core_ref, f32[1024,128]{1,0:T(8,128)} %bitcast.52, f32[8,128,128]{2,1,0:T(8,128)} %copy-done, f32[8,128,128]{2,1,0:T(8,128)} %copy-done.1, ...), custom_call_target="tpu_custom_call" | custom-call | flops 8589934592 | bytes 33554432 | tf_op jit(solution)/shard_map/main/pallas_call | solution.py:342
  69.5 0.1 collective-permute-start.1
  69.6 2.2 %collective-permute-done.1 = f32[8,152,128]{2,1,0:T(8,128)S(1)} collective-permute-done((f32[8,152,128]{2,1,0:T(8,128)}, f32[8,152,128]{2,1,0:T(8,128)S(1)}, u32[]{:S(2)}, u32[]{:S(2)}) %collective-permute-start.1) | collective-permute-done | bytes 622624 | tf_op jit(solution)/shard_map/ppermute | solution.py:32
  71.8 2.0 %add.28 = f32[8,152,128]{2,1,0:T(8,128)} add(f32[8,152,128]{2,1,0:T(8,128)} %get-tuple-element.18, f32[8,152,128]{2,1,0:T(8,128)S(1)} %collective-permute-done.1) | non-fusion elementwise | flops 155648 | bytes 1867776 | tf_op jit(solution)/shard_map/add | solution.py:384
  73.8 3.5 %all-to-all-start.1 = ((f32[8,152,128]{2,1,0:T(8,128)}), f32[8,152,128]{2,1,0:T(8,128)S(1)}, u32[]{:S(2)}, u32[]{:S(2)}) async-start(f32[8,152,128]{2,1,0:T(8,128)} %add.28), calls=%async_computation.1 | async-start | bytes 1245184 | tf_op jit(solution)/shard_map/all_to_all | solution.py:385
  77.4 0.7 fusion.6.skip_ref
  78.1 10.5 %all-to-all-done.1 = f32[8,152,128]{2,1,0:T(8,128)S(1)} async-done(((f32[8,152,128]{2,1,0:T(8,128)}), f32[8,152,128]{2,1,0:T(8,128)S(1)}, u32[]{:S(2)}, u32[]{:S(2)}) %all-to-all-start.1) | async-done | bytes 622624 | tf_op jit(solution)/shard_map/all_to_all | solution.py:385
  88.7 2.7 %collective-permute-start.2 = (f32[128,128]{1,0:T(8,128)S(1)}, f32[128,128]{1,0:T(8,128)S(1)}, u32[]{:S(2)}, u32[]{:S(2)}) collective-permute-start(f32[128,128]{1,0:T(8,128)S(1)} %slice.28), channel_id=1, source_target_pairs={{0,16},{16,0},{32,48},{48,32},{64,80},{80,64},{96,112},{112,96},{1... | collective-permute-start | bytes 196616 | tf_op jit(solution)/shard_map/ppermute | solution.py:32
  91.4 8.1 %final.1 = bf16[16,128,1024]{2,1,0:T(8,128)(2,1)} custom-call(s32[1]{0:T(128)} %bitcast.core_ref, f32[1024,128]{1,0:T(8,128)} %get-tuple-element.16.c_ref, f32[8,128,128]{2,1,0:T(8,128)} %copy-done, f32[8,128,128]{2,1,0:T(8,128)} %copy-done.1, bf16[16,128,1024]{2,1,0:T(8,128)(2,1)} %get-tuple-element.17.pg_ref, bf16[128,128]{1,0:T(8,128)(2,1)} %fusion.6.skip_ref, ...), custom_call_target="tpu_custom_call" | custom-call | flops 1073741824 | bytes 8388608 | tf_op jit(solution)/shard_map/final/pallas_call | solution.py:387
  99.5 0.7 broadcast_in_dim.25
  100.1 5.1 %all-to-all-start.2 = ((f32[8,24,128]{2,1,0:T(8,128)}), f32[8,24,128]{2,1,0:T(8,128)S(1)}, u32[]{:S(2)}, u32[]{:S(2)}) async-start(f32[8,24,128]{2,1,0:T(8,128)} %broadcast_in_dim.25), calls=%async_computation.2 | async-start | bytes 196608 | tf_op jit(solution)/shard_map/all_to_all | solution.py:25
  105.2 1.5 %collective-permute-start.3 = (f32[128,128]{1,0:T(8,128)S(1)}, f32[128,128]{1,0:T(8,128)S(1)}, u32[]{:S(2)}, u32[]{:S(2)}) collective-permute-start(f32[128,128]{1,0:T(8,128)S(1)} %slice_add_fusion), channel_id=1, source_target_pairs={{0,32},{16,48},{32,0},{48,16},{64,96},{80,112},{96,64},{112,80},{1... | collective-permute-start | bytes 196616 | tf_op jit(solution)/shard_map/ppermute | solution.py:32
  106.8 2.4 %collective-permute-start.4 = (f32[128,128]{1,0:T(8,128)S(1)}, f32[128,128]{1,0:T(8,128)S(1)}, u32[]{:S(2)}, u32[]{:S(2)}) collective-permute-start(f32[128,128]{1,0:T(8,128)S(1)} %slice_add_fusion), channel_id=1, source_target_pairs={{0,64},{16,80},{32,96},{48,112},{64,0},{80,16},{96,32},{112,48},{1... | collective-permute-start | bytes 196616 | tf_op jit(solution)/shard_map/ppermute | solution.py:32
  109.2 0.1 collective-permute-start.5
  109.2 2.8 %all-to-all-done.2 = f32[8,24,128]{2,1,0:T(8,128)S(1)} async-done(((f32[8,24,128]{2,1,0:T(8,128)}), f32[8,24,128]{2,1,0:T(8,128)S(1)}, u32[]{:S(2)}, u32[]{:S(2)}) %all-to-all-start.2) | async-done | bytes 98336 | tf_op jit(solution)/shard_map/all_to_all | solution.py:25
  112.1 0.7 broadcast_in_dim.26
  112.8 5.9 %all-to-all-start.3 = ((f32[16,24,128]{2,1,0:T(8,128)}), f32[16,24,128]{2,1,0:T(8,128)S(1)}, u32[]{:S(2)}, u32[]{:S(2)}) async-start(f32[16,24,128]{2,1,0:T(8,128)} %broadcast_in_dim.26), calls=%async_computation.3 | async-start | bytes 393216 | tf_op jit(solution)/shard_map/all_to_all | solution.py:25
  118.8 0.1 reshape.58
  118.9 0.7 copy.29
  119.6 5.8 %all-to-all-done.3 = f32[16,24,128]{2,1,0:T(8,128)S(1)} async-done(((f32[16,24,128]{2,1,0:T(8,128)}), f32[16,24,128]{2,1,0:T(8,128)S(1)}, u32[]{:S(2)}, u32[]{:S(2)}) %all-to-all-start.3) | async-done | bytes 196640 | tf_op jit(solution)/shard_map/all_to_all | solution.py:25
  125.5 0.7 bitcast_bitcast_fusion
  126.1 0.6 slice.30
  (19 shorter events, 0.2 us)
Async XLA Ops:
  16.5 17.2 %copy-start = (f32[8,128,128]{2,1,0:T(8,128)}, f32[8,128,128]{2,1,0:T(8,128)S(1)}, u32[]{:S(2)}) copy-start(f32[8,128,128]{2,1,0:T(8,128)S(1)} %all_to_all.20.mine_ref) | copy-start | bytes 1572868
  16.5 17.2 %collective-permute-start = (f32[8,128,128]{2,1,0:T(8,128)S(1)}, f32[8,128,128]{2,1,0:T(8,128)S(1)}, u32[]{:S(2)}, u32[]{:S(2)}) collective-permute-start(f32[8,128,128]{2,1,0:T(8,128)S(1)} %all_to_all.20.mine_ref), channel_id=1, source_target_pairs={{0,1},{1,0},{2,3},{3,2},{4,5},{5,4},{6,7},{7,6},{8,9},{9,8},{10,11... | collective-permute-start | bytes 1572872 | tf_op jit(solution)/shard_map/ppermute | solution.py:32
  33.7 0.8 copy-start.1
  34.5 42.8 %copy-start.2 = (bf16[64,64]{1,0:T(8,128)(2,1)S(1)}, bf16[64,64]{1,0:T(8,128)(2,1)}, u32[]{:S(2)}) copy-start(bf16[64,64]{1,0:T(8,128)(2,1)} %param.11) | copy-start | bytes 24580
  69.5 2.3 %collective-permute-start.1 = (f32[8,152,128]{2,1,0:T(8,128)}, f32[8,152,128]{2,1,0:T(8,128)S(1)}, u32[]{:S(2)}, u32[]{:S(2)}) collective-permute-start(f32[8,152,128]{2,1,0:T(8,128)} %get-tuple-element.19), channel_id=1, source_target_pairs={{0,1},{1,0},{2,3},{3,2},{4,5},{5,4},{6,7},{7,6},{8,9},{9,8},{10,11... | collective-permute-start | bytes 1867784 | tf_op jit(solution)/shard_map/ppermute | solution.py:32
  73.8 14.8 %all-to-all-start.1 = ((f32[8,152,128]{2,1,0:T(8,128)}), f32[8,152,128]{2,1,0:T(8,128)S(1)}, u32[]{:S(2)}, u32[]{:S(2)}) async-start(f32[8,152,128]{2,1,0:T(8,128)} %add.28), calls=%async_computation.1 | async-start | bytes 1245184 | tf_op jit(solution)/shard_map/all_to_all | solution.py:385
  88.7 16.6 %collective-permute-start.2 = (f32[128,128]{1,0:T(8,128)S(1)}, f32[128,128]{1,0:T(8,128)S(1)}, u32[]{:S(2)}, u32[]{:S(2)}) collective-permute-start(f32[128,128]{1,0:T(8,128)S(1)} %slice.28), channel_id=1, source_target_pairs={{0,16},{16,0},{32,48},{48,32},{64,80},{80,64},{96,112},{112,96},{1... | collective-permute-start | bytes 196616 | tf_op jit(solution)/shard_map/ppermute | solution.py:32
  100.1 12.0 %all-to-all-start.2 = ((f32[8,24,128]{2,1,0:T(8,128)}), f32[8,24,128]{2,1,0:T(8,128)S(1)}, u32[]{:S(2)}, u32[]{:S(2)}) async-start(f32[8,24,128]{2,1,0:T(8,128)} %broadcast_in_dim.25), calls=%async_computation.2 | async-start | bytes 196608 | tf_op jit(solution)/shard_map/all_to_all | solution.py:25
  105.2 13.5 %collective-permute-start.3 = (f32[128,128]{1,0:T(8,128)S(1)}, f32[128,128]{1,0:T(8,128)S(1)}, u32[]{:S(2)}, u32[]{:S(2)}) collective-permute-start(f32[128,128]{1,0:T(8,128)S(1)} %slice_add_fusion), channel_id=1, source_target_pairs={{0,32},{16,48},{32,0},{48,16},{64,96},{80,112},{96,64},{112,80},{1... | collective-permute-start | bytes 196616 | tf_op jit(solution)/shard_map/ppermute | solution.py:32
  106.8 12.0 %collective-permute-start.4 = (f32[128,128]{1,0:T(8,128)S(1)}, f32[128,128]{1,0:T(8,128)S(1)}, u32[]{:S(2)}, u32[]{:S(2)}) collective-permute-start(f32[128,128]{1,0:T(8,128)S(1)} %slice_add_fusion), channel_id=1, source_target_pairs={{0,64},{16,80},{32,96},{48,112},{64,0},{80,16},{96,32},{112,48},{1... | collective-permute-start | bytes 196616 | tf_op jit(solution)/shard_map/ppermute | solution.py:32
  109.2 9.6 %collective-permute-start.5 = (f32[128,128]{1,0:T(8,128)S(1)}, f32[128,128]{1,0:T(8,128)S(1)}, u32[]{:S(2)}, u32[]{:S(2)}) collective-permute-start(f32[128,128]{1,0:T(8,128)S(1)} %slice_add_fusion), channel_id=1, source_target_pairs={{0,96},{16,112},{32,64},{48,80},{64,32},{80,48},{96,0},{112,16},{1... | collective-permute-start | bytes 196616 | tf_op jit(solution)/shard_map/ppermute | solution.py:32
  112.8 12.6 %all-to-all-start.3 = ((f32[16,24,128]{2,1,0:T(8,128)}), f32[16,24,128]{2,1,0:T(8,128)S(1)}, u32[]{:S(2)}, u32[]{:S(2)}) async-start(f32[16,24,128]{2,1,0:T(8,128)} %broadcast_in_dim.26), calls=%async_computation.3 | async-start | bytes 393216 | tf_op jit(solution)/shard_map/all_to_all | solution.py:25

commit v3 on v2

--- a/solution.py
+++ b/solution.py
@@ -17,7 +17,7 @@
 PRE_STEP = 4
 PRE_CHUNK = 1024
 SKEW = 2
-UNROLL = 2
+UNROLL = 4
 
 
 def to_group(block, axis, groups):
@@ -104,6 +104,14 @@
         for side, ref in enumerate((mine_ref, other_ref)):
             for i in range(kept):
                 visit((chip * 2 + (core ^ side)) * kept + i, ref[chip, i * ch : (i + 1) * ch, :])
+
+
+def copies_kernel(w_ref, out_ref):
+    kept, _, ch, _ = w_ref.shape
+    for i in range(kept):
+        upper = jnp.concatenate([w_ref[i, 0], w_ref[i, 1]], axis=1)
+        for chip in range(out_ref.shape[0]):
+            out_ref[chip, i * ch : (i + 1) * ch, :] = upper
 
 
 def pre_kernel(u_ref, g_ref, ana_ref, down_t_ref, t_ref, hc_ref):
@@ -120,8 +128,8 @@
 
 
 def main_kernel(
-    core_ref, t_ref, mine_ref, other_ref, u_ref, g_ref, hc_ref, skip_t_ref, up_t_ref, up_ref,
-    down_t_ref, syn_ref,
+    core_ref, t_ref, mine_ref, other_ref, u_ref, g_ref, hc_ref, skip_ref, up_ref, down_t_ref,
+    syn_ref,
     res_ref, pg_ref, kept_ref, sent_ref, c_ref,
     m_ref, gu_ref, gd_ref, gs_ref,
 ):
@@ -148,7 +156,9 @@
 
         each_mode(core_ref[0], mine_ref, other_ref, ch, visit)
 
-    up_t, up, down_t = up_t_ref[...], up_ref[...], down_t_ref[...]
+    up = up_ref[...] * BF16(0.5)
+    up_t, down_t = up.T, down_t_ref[...]
+    skip_t = (twice(skip_ref[...].astype(F32).T) * 0.5).astype(BF16)
     chunks = length_x // CHUNK
     n = per_step * chunks * 2
     span = lambda j: slice(j % chunks * CHUNK, (j % chunks + 1) * CHUNK)
@@ -170,7 +180,7 @@
         p = j // chunks
         if j % chunks == 0:
             mixed, mixed_low = high_low(m_ref[pl.ds(base(p), 2 * MODES), :].T * 0.5)
-            lhs_pre[p] = jnp.concatenate([skip_t_ref[...], mixed, mixed_low], axis=1)
+            lhs_pre[p] = jnp.concatenate([skip_t, mixed, mixed_low], axis=1)
         rhs = jnp.concatenate([table_rows(j), syn_ref[:, span(j)]], axis=0)
         pre[j] = mm(lhs_pre[p], rhs)
 
@@ -307,8 +317,12 @@
     core_word = jnp.full((1,), core, jnp.int32)
     same_core = [[i for i in range(owners) if i % 2 == c] for c in range(2)]
 
-    upper = jnp.concatenate([spec_weight[:, 0], spec_weight[:, 1]], axis=2)
-    mine = to_group(upper.reshape(kept * ch, 2 * ch), "gz", same_core)
+    copies = pl.pallas_call(
+        copies_kernel,
+        out_shape=jax.ShapeDtypeStruct((chips, kept * ch, 2 * ch), F32),
+        name="copies",
+    )(spec_weight)
+    mine = lax.all_to_all(copies, "gz", 0, 0, axis_index_groups=same_core, tiled=True)
     other = swapped(mine, "gz", 1)
 
     def big(n, rows=2 * ch):
@@ -316,7 +330,6 @@
 
     rows = pairs * 2 * MODES
     cells = pencils * length_x
-    half = BF16(0.5)
     spectra, hidden_cot = pl.pallas_call(
         pre_kernel,
         grid=(pairs // PRE_STEP,),
@@ -350,8 +363,7 @@
             big(PER_STEP),
             big(PER_STEP),
             big(PER_STEP, 2 * hid),
-            whole((2 * ch, 2 * ch)),
-            whole((hid, ch)),
+            whole((ch, ch)),
             whole((ch, hid)),
             whole((ch, hid)),
             whole((2 * MODES, length_x)),
@@ -377,8 +389,8 @@
         ),
         name="main",
     )(
-        core_word, spectra, mine, other, u, g, hidden_cot, twice(skip_weight.T) * half,
-        up_weight.T * half, up_weight * half, down_weight.T, synthesis.T,
+        core_word, spectra, mine, other, u, g, hidden_cot, skip_weight, up_weight, down_weight.T,
+        synthesis.T,
     )
 
     chip_sum = kept_half + swapped(sent_half, "gz", 1)

time: 128 us -> 124 us (0.969)
  local copies, waits for them, and re-layouts: 6.7 us -> 4.26 us
  other arithmetic: 4.9 us -> 2.74 us
  Pallas kernels: 54.8 us -> 56.1 us
    mul x2 -> x0, other arithmetic: 2.08 us -> none  [the longest x1 1.38 us: local(): up_weight.T * half]
    pallas_call x0 -> x1, Pallas kernels: none -> 1.8 us  [local(): pl.pallas_call(copies_kernel, out_shape=jax.ShapeDtypeStruct((chips, kept...]
  transfers between devices with their start and end apart: 9 -> 9, of which waited for: 4 -> 4; matrix products, arithmetic and copies ran while one was open for 5% -> 2% of each run, Pallas kernels for 16% -> 16%
where the time goes in v3:
time: 124 us
  Pallas kernels  56.1 us (45%)
  starting transfers between devices  23.4 us (19%)
  waiting for transfers between devices  21.3 us (17%)
  blocking collectives  15.1 us (12%)
  local copies, waits for them, and re-layouts  4.26 us (3%)
  other arithmetic  2.74 us (2%)
    pallas_call x1, Pallas kernels, local(): pl.pallas_call(main_kernel, grid=(pairs // PER_STEP,), in_specs=[smem, wh...  35 us
    all_to_all x1, blocking collectives, local(): lax.all_to_all(copies, 'gz', 0, 0, axis_index_groups=same_core, tiled=True)  15.1 us
    pallas_call x1, Pallas kernels, local(): pl.pallas_call(pre_kernel, grid=(pairs // PRE_STEP,), in_specs=[big(PRE_S...  11.7 us
    all_to_all x2, starting transfers between devices, to_group(): lax.all_to_all(jnp.broadcast_to(block[None], (peers, *block.shape)), axis...  11 us
    all_to_all x1, waiting for transfers between devices, local(): lax.all_to_all(chip_sum, 'gz', 0, 0, axis_index_groups=same_core, tiled=T...  10.5 us
    ppermute x6, starting transfers between devices, swapped(): lax.ppermute(block, axis, [(i, i ^ mask) for i in range(lax.axis_size(axi...  8.81 us
    all_to_all x2, waiting for transfers between devices, to_group(): lax.all_to_all(jnp.broadcast_to(block[None], (peers, *block.shape)), axis...  8.69 us
    pallas_call x1, Pallas kernels, local(): pl.pallas_call(final_kernel, grid=(pairs // FINAL_STEP,), in_specs=[smem,...  7.6 us
  transfers between devices with their start and end apart: 9, of which 4 were waited for; matrix products, arithmetic and copies ran while one was open for 2% of the time, Pallas kernels for 16%

profile of v3, /device:TPU:1, one launch (start us, length us, event | category | flops | bytes accessed | tf_op | source)
XLA Modules:
  0.0 123.6 jit_solution(12947877410393568286)
XLA Ops:
  0.6 1.8 %copies.1 = f32[8,128,128]{2,1,0:T(8,128)} custom-call(f32[2,2,64,64]{3,2,1,0:T(8,128)} %w_ref.1), custom_call_target="tpu_custom_call" | custom-call | tf_op jit(solution)/shard_map/copies/pallas_call | solution.py:320
  2.4 15.1 %all_to_all.20.mine_ref = f32[8,128,128]{2,1,0:T(8,128)S(1)} all-to-all(f32[8,128,128]{2,1,0:T(8,128)} %copies.1), channel_id=1, replica_groups={{0,2,4,6,8,10,12,14},{1,3,5,7,9,11,13,15},{16,18,20,22,24,26,28,30},{17..., dimensions={0} | all-to-all | bytes 1048576 | tf_op jit(solution)/shard_map/all_to_all | solution.py:325
  17.5 1.8 %collective-permute-start = (f32[8,128,128]{2,1,0:T(8,128)S(1)}, f32[8,128,128]{2,1,0:T(8,128)S(1)}, u32[]{:S(2)}, u32[]{:S(2)}) collective-permute-start(f32[8,128,128]{2,1,0:T(8,128)S(1)} %all_to_all.20.mine_ref), channel_id=1, source_target_pairs={{0,1},{1,0},{2,3},{3,2},{4,5},{5,4},{6,7},{7,6},{8,9},{9,8},{10,11... | collective-permute-start | bytes 1572872 | tf_op jit(solution)/shard_map/ppermute | solution.py:32
  19.3 11.7 %pre.1 = (f32[16,64,128]{2,1,0:T(8,128)}, bf16[16,512,1024]{2,1,0:T(8,128)(2,1)}) custom-call(bf16[16,128,1024]{2,1,0:T(8,128)(2,1)} %bitcast.32, bf16[16,128,1024]{2,1,0:T(8,128)(2,1)} %bitcast.34, bf16[1024,64]{1,0:T(8,128)(2,1)} %constant.31.clone.ana_ref, bf16[64,256]{1,0:T(8,128)(2,1)} %bitcast.39), custom_call_target="tpu_custom_call" | custom-call | flops 1342177280 | bytes 25165824 | tf_op jit(solution)/shard_map/pre/pallas_call | solution.py:333
  31.1 0.0 collective-permute-done.other_ref
  31.1 0.8 copy-done.1
  31.9 35.0 %main.1 = (bf16[16,128,1024]{2,1,0:T(8,128)(2,1)}, bf16[16,128,1024]{2,1,0:T(8,128)(2,1)}, f32[8,152,128]{2,1,0:T(8,128)}, f32[8,152,128]{2,1,0:T(8,128)}, f32[1024,128]{1,0:T(8,128)}) custom-call(s32[1]{0:T(128)} %bitcast.core_ref, f32[1024,128]{1,0:T(8,128)} %bitcast.42, f32[8,128,128]{2,1,0:T(8,128)} %copy-done, f32[8,128,128]{2,1,0:T(8,128)} %copy-done.1, ...), custom_call_target="tpu_custom_call" | custom-call | flops 8589934592 | bytes 33554432 | tf_op jit(solution)/shard_map/main/pallas_call | solution.py:355
  66.9 0.3 collective-permute-start.1
  67.1 2.1 %collective-permute-done.1 = f32[8,152,128]{2,1,0:T(8,128)S(1)} collective-permute-done((f32[8,152,128]{2,1,0:T(8,128)}, f32[8,152,128]{2,1,0:T(8,128)S(1)}, u32[]{:S(2)}, u32[]{:S(2)}) %collective-permute-start.1) | collective-permute-done | bytes 622624 | tf_op jit(solution)/shard_map/ppermute | solution.py:32
  69.2 2.0 %add.24 = f32[8,152,128]{2,1,0:T(8,128)} add(f32[8,152,128]{2,1,0:T(8,128)} %get-tuple-element.18, f32[8,152,128]{2,1,0:T(8,128)S(1)} %collective-permute-done.1) | non-fusion elementwise | flops 155648 | bytes 1867776 | tf_op jit(solution)/shard_map/add | solution.py:396
  71.2 3.5 %all-to-all-start.1 = ((f32[8,152,128]{2,1,0:T(8,128)}), f32[8,152,128]{2,1,0:T(8,128)S(1)}, u32[]{:S(2)}, u32[]{:S(2)}) async-start(f32[8,152,128]{2,1,0:T(8,128)} %add.24), calls=%async_computation.1 | async-start | bytes 1245184 | tf_op jit(solution)/shard_map/all_to_all | solution.py:397
  74.7 0.7 fusion.2.skip_ref
  75.4 10.5 %all-to-all-done.1 = f32[8,152,128]{2,1,0:T(8,128)S(1)} async-done(((f32[8,152,128]{2,1,0:T(8,128)}), f32[8,152,128]{2,1,0:T(8,128)S(1)}, u32[]{:S(2)}, u32[]{:S(2)}) %all-to-all-start.1) | async-done | bytes 622624 | tf_op jit(solution)/shard_map/all_to_all | solution.py:397
  86.0 2.7 %collective-permute-start.2 = (f32[128,128]{1,0:T(8,128)S(1)}, f32[128,128]{1,0:T(8,128)S(1)}, u32[]{:S(2)}, u32[]{:S(2)}) collective-permute-start(f32[128,128]{1,0:T(8,128)S(1)} %slice.20), channel_id=1, source_target_pairs={{0,16},{16,0},{32,48},{48,32},{64,80},{80,64},{96,112},{112,96},{1... | collective-permute-start | bytes 196616 | tf_op jit(solution)/shard_map/ppermute | solution.py:32
  88.7 7.6 %final.1 = bf16[16,128,1024]{2,1,0:T(8,128)(2,1)} custom-call(s32[1]{0:T(128)} %bitcast.core_ref, f32[1024,128]{1,0:T(8,128)} %get-tuple-element.16.c_ref, f32[8,128,128]{2,1,0:T(8,128)} %copy-done, f32[8,128,128]{2,1,0:T(8,128)} %copy-done.1, bf16[16,128,1024]{2,1,0:T(8,128)(2,1)} %get-tuple-element.17.pg_ref, bf16[128,128]{1,0:T(8,128)(2,1)} %fusion.2.skip_ref, ...), custom_call_target="tpu_custom_call" | custom-call | flops 1073741824 | bytes 8388608 | tf_op jit(solution)/shard_map/final/pallas_call | solution.py:399
  96.3 0.7 broadcast_in_dim.7
  97.0 5.1 %all-to-all-start.2 = ((f32[8,24,128]{2,1,0:T(8,128)}), f32[8,24,128]{2,1,0:T(8,128)S(1)}, u32[]{:S(2)}, u32[]{:S(2)}) async-start(f32[8,24,128]{2,1,0:T(8,128)} %broadcast_in_dim.7), calls=%async_computation.2 | async-start | bytes 196608 | tf_op jit(solution)/shard_map/all_to_all | solution.py:25
  102.1 0.0 collective-permute-done.2
  102.1 1.5 %collective-permute-start.3 = (f32[128,128]{1,0:T(8,128)S(1)}, f32[128,128]{1,0:T(8,128)S(1)}, u32[]{:S(2)}, u32[]{:S(2)}) collective-permute-start(f32[128,128]{1,0:T(8,128)S(1)} %slice_add_fusion), channel_id=1, source_target_pairs={{0,32},{16,48},{32,0},{48,16},{64,96},{80,112},{96,64},{112,80},{1... | collective-permute-start | bytes 196616 | tf_op jit(solution)/shard_map/ppermute | solution.py:32
  103.6 2.4 %collective-permute-start.4 = (f32[128,128]{1,0:T(8,128)S(1)}, f32[128,128]{1,0:T(8,128)S(1)}, u32[]{:S(2)}, u32[]{:S(2)}) collective-permute-start(f32[128,128]{1,0:T(8,128)S(1)} %slice_add_fusion), channel_id=1, source_target_pairs={{0,64},{16,80},{32,96},{48,112},{64,0},{80,16},{96,32},{112,48},{1... | collective-permute-start | bytes 196616 | tf_op jit(solution)/shard_map/ppermute | solution.py:32
  106.0 0.1 collective-permute-start.5
  106.1 2.8 %all-to-all-done.2 = f32[8,24,128]{2,1,0:T(8,128)S(1)} async-done(((f32[8,24,128]{2,1,0:T(8,128)}), f32[8,24,128]{2,1,0:T(8,128)S(1)}, u32[]{:S(2)}, u32[]{:S(2)}) %all-to-all-start.2) | async-done | bytes 98336 | tf_op jit(solution)/shard_map/all_to_all | solution.py:25
  109.0 0.7 broadcast_in_dim.8
  109.7 5.9 %all-to-all-start.3 = ((f32[16,24,128]{2,1,0:T(8,128)}), f32[16,24,128]{2,1,0:T(8,128)S(1)}, u32[]{:S(2)}, u32[]{:S(2)}) async-start(f32[16,24,128]{2,1,0:T(8,128)} %broadcast_in_dim.8), calls=%async_computation.3 | async-start | bytes 393216 | tf_op jit(solution)/shard_map/all_to_all | solution.py:25
  115.6 0.0 collective-permute-done.3
  115.6 0.0 collective-permute-done.4
  115.6 0.0 collective-permute-done.5
  115.6 0.1 reshape.54
  115.8 0.7 copy.21
  116.4 5.8 %all-to-all-done.3 = f32[16,24,128]{2,1,0:T(8,128)S(1)} async-done(((f32[16,24,128]{2,1,0:T(8,128)}), f32[16,24,128]{2,1,0:T(8,128)S(1)}, u32[]{:S(2)}, u32[]{:S(2)}) %all-to-all-start.3) | async-done | bytes 196640 | tf_op jit(solution)/shard_map/all_to_all | solution.py:25
  122.3 0.7 bitcast_bitcast_fusion
  123.0 0.6 slice.22
  (13 shorter events, 0.1 us)
Async XLA Ops:
  17.5 13.6 %copy-start = (f32[8,128,128]{2,1,0:T(8,128)}, f32[8,128,128]{2,1,0:T(8,128)S(1)}, u32[]{:S(2)}) copy-start(f32[8,128,128]{2,1,0:T(8,128)S(1)} %all_to_all.20.mine_ref) | copy-start | bytes 1572868
  17.5 13.6 %collective-permute-start = (f32[8,128,128]{2,1,0:T(8,128)S(1)}, f32[8,128,128]{2,1,0:T(8,128)S(1)}, u32[]{:S(2)}, u32[]{:S(2)}) collective-permute-start(f32[8,128,128]{2,1,0:T(8,128)S(1)} %all_to_all.20.mine_ref), channel_id=1, source_target_pairs={{0,1},{1,0},{2,3},{3,2},{4,5},{5,4},{6,7},{7,6},{8,9},{9,8},{10,11... | collective-permute-start | bytes 1572872 | tf_op jit(solution)/shard_map/ppermute | solution.py:32
  31.1 0.8 copy-start.1
  31.9 42.8 %copy-start.2 = (bf16[64,64]{1,0:T(8,128)(2,1)S(1)}, bf16[64,64]{1,0:T(8,128)(2,1)}, u32[]{:S(2)}) copy-start(bf16[64,64]{1,0:T(8,128)(2,1)} %skip_ref.1) | copy-start | bytes 24580
  66.9 2.3 %collective-permute-start.1 = (f32[8,152,128]{2,1,0:T(8,128)}, f32[8,152,128]{2,1,0:T(8,128)S(1)}, u32[]{:S(2)}, u32[]{:S(2)}) collective-permute-start(f32[8,152,128]{2,1,0:T(8,128)} %get-tuple-element.19), channel_id=1, source_target_pairs={{0,1},{1,0},{2,3},{3,2},{4,5},{5,4},{6,7},{7,6},{8,9},{9,8},{10,11... | collective-permute-start | bytes 1867784 | tf_op jit(solution)/shard_map/ppermute | solution.py:32
  71.2 14.8 %all-to-all-start.1 = ((f32[8,152,128]{2,1,0:T(8,128)}), f32[8,152,128]{2,1,0:T(8,128)S(1)}, u32[]{:S(2)}, u32[]{:S(2)}) async-start(f32[8,152,128]{2,1,0:T(8,128)} %add.24), calls=%async_computation.1 | async-start | bytes 1245184 | tf_op jit(solution)/shard_map/all_to_all | solution.py:397
  86.0 16.1 %collective-permute-start.2 = (f32[128,128]{1,0:T(8,128)S(1)}, f32[128,128]{1,0:T(8,128)S(1)}, u32[]{:S(2)}, u32[]{:S(2)}) collective-permute-start(f32[128,128]{1,0:T(8,128)S(1)} %slice.20), channel_id=1, source_target_pairs={{0,16},{16,0},{32,48},{48,32},{64,80},{80,64},{96,112},{112,96},{1... | collective-permute-start | bytes 196616 | tf_op jit(solution)/shard_map/ppermute | solution.py:32
  97.0 12.0 %all-to-all-start.2 = ((f32[8,24,128]{2,1,0:T(8,128)}), f32[8,24,128]{2,1,0:T(8,128)S(1)}, u32[]{:S(2)}, u32[]{:S(2)}) async-start(f32[8,24,128]{2,1,0:T(8,128)} %broadcast_in_dim.7), calls=%async_computation.2 | async-start | bytes 196608 | tf_op jit(solution)/shard_map/all_to_all | solution.py:25
  102.1 13.5 %collective-permute-start.3 = (f32[128,128]{1,0:T(8,128)S(1)}, f32[128,128]{1,0:T(8,128)S(1)}, u32[]{:S(2)}, u32[]{:S(2)}) collective-permute-start(f32[128,128]{1,0:T(8,128)S(1)} %slice_add_fusion), channel_id=1, source_target_pairs={{0,32},{16,48},{32,0},{48,16},{64,96},{80,112},{96,64},{112,80},{1... | collective-permute-start | bytes 196616 | tf_op jit(solution)/shard_map/ppermute | solution.py:32
  103.6 12.0 %collective-permute-start.4 = (f32[128,128]{1,0:T(8,128)S(1)}, f32[128,128]{1,0:T(8,128)S(1)}, u32[]{:S(2)}, u32[]{:S(2)}) collective-permute-start(f32[128,128]{1,0:T(8,128)S(1)} %slice_add_fusion), channel_id=1, source_target_pairs={{0,64},{16,80},{32,96},{48,112},{64,0},{80,16},{96,32},{112,48},{1... | collective-permute-start | bytes 196616 | tf_op jit(solution)/shard_map/ppermute | solution.py:32
  106.0 9.6 %collective-permute-start.5 = (f32[128,128]{1,0:T(8,128)S(1)}, f32[128,128]{1,0:T(8,128)S(1)}, u32[]{:S(2)}, u32[]{:S(2)}) collective-permute-start(f32[128,128]{1,0:T(8,128)S(1)} %slice_add_fusion), channel_id=1, source_target_pairs={{0,96},{16,112},{32,64},{48,80},{64,32},{80,48},{96,0},{112,16},{1... | collective-permute-start | bytes 196616 | tf_op jit(solution)/shard_map/ppermute | solution.py:32
  109.7 12.6 %all-to-all-start.3 = ((f32[16,24,128]{2,1,0:T(8,128)}), f32[16,24,128]{2,1,0:T(8,128)S(1)}, u32[]{:S(2)}, u32[]{:S(2)}) async-start(f32[16,24,128]{2,1,0:T(8,128)} %broadcast_in_dim.8), calls=%async_computation.3 | async-start | bytes 393216 | tf_op jit(solution)/shard_map/all_to_all | solution.py:25

commit v4 on v3

--- a/solution.py
+++ b/solution.py
@@ -18,6 +18,9 @@
 PRE_CHUNK = 1024
 SKEW = 2
 UNROLL = 4
+PRE_MIB = 50
+MAIN_MIB = 50
+FINAL_MIB = 50
 
 
 def to_group(block, axis, groups):
@@ -345,6 +348,7 @@
         cost_estimate=pl.CostEstimate(
             flops=2 * cells * ch * (hid + 2 * MODES), bytes_accessed=cells * 12 * ch, transcendentals=0
         ),
+        compiler_params=pltpu.CompilerParams(vmem_limit_bytes=PRE_MIB << 20),
         name="pre",
     )(u, g, analysis, down_weight.T)
     spectra = spectra.reshape(rows, 2 * ch)
@@ -387,6 +391,7 @@
         cost_estimate=pl.CostEstimate(
             flops=16 * cells * ch * hid, bytes_accessed=cells * 16 * ch, transcendentals=cells * hid
         ),
+        compiler_params=pltpu.CompilerParams(vmem_limit_bytes=MAIN_MIB << 20),
         name="main",
     )(
         core_word, spectra, mine, other, u, g, hidden_cot, skip_weight, up_weight, down_weight.T,
@@ -414,6 +419,7 @@
         cost_estimate=pl.CostEstimate(
             flops=8 * cells * ch * ch, bytes_accessed=cells * 4 * ch, transcendentals=0
         ),
+        compiler_params=pltpu.CompilerParams(vmem_limit_bytes=FINAL_MIB << 20),
         name="final",
     )(core_word, coeffs, mine, other, pre_grad, twice(skip_weight), analysis.T)
 

time: 124 us -> 122 us (0.984)
  Pallas kernels: 56.1 us -> 54.1 us
  other arithmetic: 2.74 us -> 1.05 us
    pallas_call x1, Pallas kernels: 35 us -> 33.5 us  [local(): pl.pallas_call(main_kernel, grid=(pairs // PER_STEP,), in_specs=[smem, wh...]
where the time goes in v4:
time: 122 us; the launch traced here: 121 us
  Pallas kernels  54.1 us (44%)
  starting transfers between devices  23.1 us (19%)
  waiting for transfers between devices  21.9 us (18%)
  blocking collectives  15.1 us (12%)
  local copies, waits for them, and re-layouts  5.15 us (4%)
    pallas_call x1, Pallas kernels, local(): pl.pallas_call(main_kernel, grid=(pairs // PER_STEP,), in_specs=[smem, wh...  33.5 us
    all_to_all x1, blocking collectives, local(): lax.all_to_all(copies, 'gz', 0, 0, axis_index_groups=same_core, tiled=True)  15.1 us
    pallas_call x1, Pallas kernels, local(): pl.pallas_call(pre_kernel, grid=(pairs // PRE_STEP,), in_specs=[big(PRE_S...  11.8 us
    all_to_all x1, waiting for transfers between devices, local(): lax.all_to_all(chip_sum, 'gz', 0, 0, axis_index_groups=same_core, tiled=T...  11.2 us
    all_to_all x2, starting transfers between devices, to_group(): lax.all_to_all(jnp.broadcast_to(block[None], (peers, *block.shape)), axis...  11 us
    all_to_all x2, waiting for transfers between devices, to_group(): lax.all_to_all(jnp.broadcast_to(block[None], (peers, *block.shape)), axis...  8.69 us
    ppermute x6, starting transfers between devices, swapped(): lax.ppermute(block, axis, [(i, i ^ mask) for i in range(lax.axis_size(axi...  8.52 us
    pallas_call x1, Pallas kernels, local(): pl.pallas_call(final_kernel, grid=(pairs // FINAL_STEP,), in_specs=[smem,...  7.11 us
  transfers between devices with their start and end apart: 9, of which 4 were waited for; matrix products, arithmetic and copies ran while one was open for 2% of the time, Pallas kernels for 16%

profile of v4, /device:TPU:1, one launch (start us, length us, event | category | flops | bytes accessed | tf_op | source)
XLA Modules:
  0.0 121.2 jit_solution(16183527676376983871)
XLA Ops:
  0.6 1.8 %copies.1 = f32[8,128,128]{2,1,0:T(8,128)} custom-call(f32[2,2,64,64]{3,2,1,0:T(8,128)} %w_ref.1), custom_call_target="tpu_custom_call" | custom-call | tf_op jit(solution)/shard_map/copies/pallas_call | solution.py:323
  2.4 15.1 %all_to_all.20.mine_ref = f32[8,128,128]{2,1,0:T(8,128)S(1)} all-to-all(f32[8,128,128]{2,1,0:T(8,128)} %copies.1), channel_id=1, replica_groups={{0,2,4,6,8,10,12,14},{1,3,5,7,9,11,13,15},{16,18,20,22,24,26,28,30},{17..., dimensions={0} | all-to-all | bytes 1048576 | tf_op jit(solution)/shard_map/all_to_all | solution.py:328
  17.5 1.8 %collective-permute-start = (f32[8,128,128]{2,1,0:T(8,128)S(1)}, f32[8,128,128]{2,1,0:T(8,128)S(1)}, u32[]{:S(2)}, u32[]{:S(2)}) collective-permute-start(f32[8,128,128]{2,1,0:T(8,128)S(1)} %all_to_all.20.mine_ref), channel_id=1, source_target_pairs={{0,1},{1,0},{2,3},{3,2},{4,5},{5,4},{6,7},{7,6},{8,9},{9,8},{10,11... | collective-permute-start | bytes 1572872 | tf_op jit(solution)/shard_map/ppermute | solution.py:35
  19.3 0.9 copy-done
  20.3 0.8 copy-done.2
  21.0 11.8 %pre.1 = (f32[16,64,128]{2,1,0:T(8,128)S(1)}, bf16[16,512,1024]{2,1,0:T(8,128)(2,1)}) custom-call(bf16[16,128,1024]{2,1,0:T(8,128)(2,1)} %bitcast.35, bf16[16,128,1024]{2,1,0:T(8,128)(2,1)} %bitcast.37, bf16[1024,64]{1,0:T(8,128)(2,1)S(1)} %copy-done, bf16[64,256]{1,0:T(8,128)(2,1)S(1)} %bitcast.31), custom_call_target="tpu_custom_call" | custom-call | flops 1342177280 | bytes 25165824 | tf_op jit(solution)/shard_map/pre/pallas_call | solution.py:336
  32.8 0.0 collective-permute-done.other_ref
  32.8 0.0 copy-start.1
  32.8 33.5 %main.1 = (bf16[16,128,1024]{2,1,0:T(8,128)(2,1)}, bf16[16,128,1024]{2,1,0:T(8,128)(2,1)}, f32[8,152,128]{2,1,0:T(8,128)S(1)}, f32[8,152,128]{2,1,0:T(8,128)S(1)}, f32[1024,128]{1,0:T(8,128)S(1)}) custom-call(s32[1]{0:T(128)} %bitcast.core_ref, f32[1024,128]{1,0:T(8,128)S(1)} %bitcast.33, f32[8,128,128]{2,1,0:T(8,128)S(1)} %all_to_all.20.mine_ref, ...), custom_call_target="tpu_custom_call" | custom-call | flops 8589934592 | bytes 33554432 | tf_op jit(solution)/shard_map/main/pallas_call | solution.py:359
  66.3 0.0 collective-permute-start.1
  66.3 2.0 %collective-permute-done.1 = f32[8,152,128]{2,1,0:T(8,128)S(1)} collective-permute-done((f32[8,152,128]{2,1,0:T(8,128)S(1)}, f32[8,152,128]{2,1,0:T(8,128)S(1)}, u32[]{:S(2)}, u32[]{:S(2)}) %collective-permute-start.1) | collective-permute-done | bytes 622624 | tf_op jit(solution)/shard_map/ppermute | solution.py:35
  68.4 0.9 add.24
  69.2 3.5 %all-to-all-start.1 = ((f32[8,152,128]{2,1,0:T(8,128)}), f32[8,152,128]{2,1,0:T(8,128)S(1)}, u32[]{:S(2)}, u32[]{:S(2)}) async-start(f32[8,152,128]{2,1,0:T(8,128)} %add.24), calls=%async_computation.1 | async-start | bytes 1245184 | tf_op jit(solution)/shard_map/all_to_all | solution.py:402
  72.8 0.1 fusion.2.skip_ref
  72.9 11.2 %all-to-all-done.1 = f32[8,152,128]{2,1,0:T(8,128)S(1)} async-done(((f32[8,152,128]{2,1,0:T(8,128)}), f32[8,152,128]{2,1,0:T(8,128)S(1)}, u32[]{:S(2)}, u32[]{:S(2)}) %all-to-all-start.1) | async-done | bytes 622624 | tf_op jit(solution)/shard_map/all_to_all | solution.py:402
  84.1 2.7 %collective-permute-start.2 = (f32[128,128]{1,0:T(8,128)S(1)}, f32[128,128]{1,0:T(8,128)S(1)}, u32[]{:S(2)}, u32[]{:S(2)}) collective-permute-start(f32[128,128]{1,0:T(8,128)S(1)} %slice.20), channel_id=1, source_target_pairs={{0,16},{16,0},{32,48},{48,32},{64,80},{80,64},{96,112},{112,96},{1... | collective-permute-start | bytes 196616 | tf_op jit(solution)/shard_map/ppermute | solution.py:35
  86.8 7.1 %final.1 = bf16[16,128,1024]{2,1,0:T(8,128)(2,1)} custom-call(s32[1]{0:T(128)} %bitcast.core_ref, f32[1024,128]{1,0:T(8,128)S(1)} %get-tuple-element.16.c_ref, f32[8,128,128]{2,1,0:T(8,128)S(1)} %all_to_all.20.mine_ref, f32[8,128,128]{2,1,0:T(8,128)S(1)} %collective-permute-done.other_ref, bf16[16,128,1024]{2,1,0:T(8,128)(2,1)} %get-tuple-element.17.pg_ref, ...), custom_call_target="tpu_custom_call" | custom-call | flops 1073741824 | bytes 8388608 | tf_op jit(solution)/shard_map/final/pallas_call | solution.py:404
  93.9 0.7 broadcast_in_dim.7
  94.5 5.1 %all-to-all-start.2 = ((f32[8,24,128]{2,1,0:T(8,128)}), f32[8,24,128]{2,1,0:T(8,128)S(1)}, u32[]{:S(2)}, u32[]{:S(2)}) async-start(f32[8,24,128]{2,1,0:T(8,128)} %broadcast_in_dim.7), calls=%async_computation.2 | async-start | bytes 196608 | tf_op jit(solution)/shard_map/all_to_all | solution.py:28
  99.7 0.0 collective-permute-done.2
  99.7 1.5 %collective-permute-start.3 = (f32[128,128]{1,0:T(8,128)S(1)}, f32[128,128]{1,0:T(8,128)S(1)}, u32[]{:S(2)}, u32[]{:S(2)}) collective-permute-start(f32[128,128]{1,0:T(8,128)S(1)} %slice_add_fusion), channel_id=1, source_target_pairs={{0,32},{16,48},{32,0},{48,16},{64,96},{80,112},{96,64},{112,80},{1... | collective-permute-start | bytes 196616 | tf_op jit(solution)/shard_map/ppermute | solution.py:35
  101.2 2.4 %collective-permute-start.4 = (f32[128,128]{1,0:T(8,128)S(1)}, f32[128,128]{1,0:T(8,128)S(1)}, u32[]{:S(2)}, u32[]{:S(2)}) collective-permute-start(f32[128,128]{1,0:T(8,128)S(1)} %slice_add_fusion), channel_id=1, source_target_pairs={{0,64},{16,80},{32,96},{48,112},{64,0},{80,16},{96,32},{112,48},{1... | collective-permute-start | bytes 196616 | tf_op jit(solution)/shard_map/ppermute | solution.py:35
  103.6 0.1 collective-permute-start.5
  103.7 2.8 %all-to-all-done.2 = f32[8,24,128]{2,1,0:T(8,128)S(1)} async-done(((f32[8,24,128]{2,1,0:T(8,128)}), f32[8,24,128]{2,1,0:T(8,128)S(1)}, u32[]{:S(2)}, u32[]{:S(2)}) %all-to-all-start.2) | async-done | bytes 98336 | tf_op jit(solution)/shard_map/all_to_all | solution.py:28
  106.6 0.7 broadcast_in_dim.8
  107.3 5.9 %all-to-all-start.3 = ((f32[16,24,128]{2,1,0:T(8,128)}), f32[16,24,128]{2,1,0:T(8,128)S(1)}, u32[]{:S(2)}, u32[]{:S(2)}) async-start(f32[16,24,128]{2,1,0:T(8,128)} %broadcast_in_dim.8), calls=%async_computation.3 | async-start | bytes 393216 | tf_op jit(solution)/shard_map/all_to_all | solution.py:28
  113.2 0.0 collective-permute-done.4
  113.2 0.1 reshape.54
  113.4 0.7 copy.21
  114.0 5.8 %all-to-all-done.3 = f32[16,24,128]{2,1,0:T(8,128)S(1)} async-done(((f32[16,24,128]{2,1,0:T(8,128)}), f32[16,24,128]{2,1,0:T(8,128)S(1)}, u32[]{:S(2)}, u32[]{:S(2)}) %all-to-all-start.3) | async-done | bytes 196640 | tf_op jit(solution)/shard_map/all_to_all | solution.py:28
  119.9 0.7 bitcast_bitcast_fusion
  120.5 0.6 slice.22
  (21 shorter events, 0.1 us)
Async XLA Ops:
  17.5 15.3 %collective-permute-start = (f32[8,128,128]{2,1,0:T(8,128)S(1)}, f32[8,128,128]{2,1,0:T(8,128)S(1)}, u32[]{:S(2)}, u32[]{:S(2)}) collective-permute-start(f32[8,128,128]{2,1,0:T(8,128)S(1)} %all_to_all.20.mine_ref), channel_id=1, source_target_pairs={{0,1},{1,0},{2,3},{3,2},{4,5},{5,4},{6,7},{7,6},{8,9},{9,8},{10,11... | collective-permute-start | bytes 1572872 | tf_op jit(solution)/shard_map/ppermute | solution.py:35
  19.3 0.9 copy-start
  20.3 0.8 copy-start.2
  21.0 11.8 %copy-start.3 = (bf16[256,64]{0,1:T(8,128)(2,1)S(1)}, bf16[256,64]{0,1:T(8,128)(2,1)}, u32[]{:S(2)}) copy-start(bf16[256,64]{0,1:T(8,128)(2,1)} %param.13) | copy-start | bytes 98308
  21.0 11.8 %copy-start.4 = (bf16[64,64]{1,0:T(8,128)(2,1)S(1)}, bf16[64,64]{1,0:T(8,128)(2,1)}, u32[]{:S(2)}) copy-start(bf16[64,64]{1,0:T(8,128)(2,1)} %skip_ref.1) | copy-start | bytes 24580
  21.0 11.8 %copy-start.5 = (bf16[64,256]{1,0:T(8,128)(2,1)S(1)}, bf16[64,256]{1,0:T(8,128)(2,1)}, u32[]{:S(2)}) copy-start(bf16[64,256]{1,0:T(8,128)(2,1)} %up_ref.1) | copy-start | bytes 98308
  21.0 11.8 %copy-start.6 = (bf16[64,1024]{1,0:T(8,128)(2,1)S(1)}, bf16[64,1024]{1,0:T(8,128)(2,1)}, u32[]{:S(2)}) copy-start(bf16[64,1024]{1,0:T(8,128)(2,1)} %constant.32.clone.syn_ref) | copy-start | bytes 393220
  32.8 54.0 %copy-start.1 = (bf16[64,1024]{1,0:T(8,128)(2,1)S(1)}, bf16[64,1024]{1,0:T(8,128)(2,1)}, u32[]{:S(2)}) copy-start(bf16[64,1024]{1,0:T(8,128)(2,1)} %constant.33.clone.ana_ref) | copy-start | bytes 393220
  66.3 2.1 %collective-permute-start.1 = (f32[8,152,128]{2,1,0:T(8,128)S(1)}, f32[8,152,128]{2,1,0:T(8,128)S(1)}, u32[]{:S(2)}, u32[]{:S(2)}) collective-permute-start(f32[8,152,128]{2,1,0:T(8,128)S(1)} %get-tuple-element.19), channel_id=1, source_target_pairs={{0,1},{1,0},{2,3},{3,2},{4,5},{5,4},{6,7},{7,6},{8,9},{9,8},{10,11... | collective-permute-start | bytes 1867784 | tf_op jit(solution)/shard_map/ppermute | solution.py:35
  69.2 14.8 %all-to-all-start.1 = ((f32[8,152,128]{2,1,0:T(8,128)}), f32[8,152,128]{2,1,0:T(8,128)S(1)}, u32[]{:S(2)}, u32[]{:S(2)}) async-start(f32[8,152,128]{2,1,0:T(8,128)} %add.24), calls=%async_computation.1 | async-start | bytes 1245184 | tf_op jit(solution)/shard_map/all_to_all | solution.py:402
  84.1 15.6 %collective-permute-start.2 = (f32[128,128]{1,0:T(8,128)S(1)}, f32[128,128]{1,0:T(8,128)S(1)}, u32[]{:S(2)}, u32[]{:S(2)}) collective-permute-start(f32[128,128]{1,0:T(8,128)S(1)} %slice.20), channel_id=1, source_target_pairs={{0,16},{16,0},{32,48},{48,32},{64,80},{80,64},{96,112},{112,96},{1... | collective-permute-start | bytes 196616 | tf_op jit(solution)/shard_map/ppermute | solution.py:35
  94.5 12.0 %all-to-all-start.2 = ((f32[8,24,128]{2,1,0:T(8,128)}), f32[8,24,128]{2,1,0:T(8,128)S(1)}, u32[]{:S(2)}, u32[]{:S(2)}) async-start(f32[8,24,128]{2,1,0:T(8,128)} %broadcast_in_dim.7), calls=%async_computation.2 | async-start | bytes 196608 | tf_op jit(solution)/shard_map/all_to_all | solution.py:28
  99.7 13.5 %collective-permute-start.3 = (f32[128,128]{1,0:T(8,128)S(1)}, f32[128,128]{1,0:T(8,128)S(1)}, u32[]{:S(2)}, u32[]{:S(2)}) collective-permute-start(f32[128,128]{1,0:T(8,128)S(1)} %slice_add_fusion), channel_id=1, source_target_pairs={{0,32},{16,48},{32,0},{48,16},{64,96},{80,112},{96,64},{112,80},{1... | collective-permute-start | bytes 196616 | tf_op jit(solution)/shard_map/ppermute | solution.py:35
  101.2 12.0 %collective-permute-start.4 = (f32[128,128]{1,0:T(8,128)S(1)}, f32[128,128]{1,0:T(8,128)S(1)}, u32[]{:S(2)}, u32[]{:S(2)}) collective-permute-start(f32[128,128]{1,0:T(8,128)S(1)} %slice_add_fusion), channel_id=1, source_target_pairs={{0,64},{16,80},{32,96},{48,112},{64,0},{80,16},{96,32},{112,48},{1... | collective-permute-start | bytes 196616 | tf_op jit(solution)/shard_map/ppermute | solution.py:35
  103.6 9.6 %collective-permute-start.5 = (f32[128,128]{1,0:T(8,128)S(1)}, f32[128,128]{1,0:T(8,128)S(1)}, u32[]{:S(2)}, u32[]{:S(2)}) collective-permute-start(f32[128,128]{1,0:T(8,128)S(1)} %slice_add_fusion), channel_id=1, source_target_pairs={{0,96},{16,112},{32,64},{48,80},{64,32},{80,48},{96,0},{112,16},{1... | collective-permute-start | bytes 196616 | tf_op jit(solution)/shard_map/ppermute | solution.py:35
  107.3 12.6 %all-to-all-start.3 = ((f32[16,24,128]{2,1,0:T(8,128)}), f32[16,24,128]{2,1,0:T(8,128)S(1)}, u32[]{:S(2)}, u32[]{:S(2)}) async-start(f32[16,24,128]{2,1,0:T(8,128)} %broadcast_in_dim.8), calls=%async_computation.3 | async-start | bytes 393216 | tf_op jit(solution)/shard_map/all_to_all | solution.py:28

commit v5 on v4

--- a/solution.py
+++ b/solution.py
@@ -18,7 +18,7 @@
 PRE_CHUNK = 1024
 SKEW = 2
 UNROLL = 4
-PRE_MIB = 50
+PRE_MIB = 60
 MAIN_MIB = 50
 FINAL_MIB = 50
 
@@ -291,6 +291,24 @@
         lhs = jnp.concatenate([skip_ref[...], back, back_low], axis=1)
         rhs = jnp.concatenate([pg_ref[p], ana_ref[...], ana_ref[...]], axis=0)
         out_ref[p] = mm(lhs, rhs).astype(BF16)
+
+
+def unpack_kernel(scale, a_ref, b_ref, c_ref, d_ref, small_ref, spec_ref, skip_ref, up_ref, down_ref):
+    spec = (a_ref[...] + b_ref[...] + c_ref[...] + d_ref[...]) * scale
+    kept, _, ch, _ = spec_ref.shape
+    for i in range(kept):
+        for r in range(2):
+            spec_ref[i, r] = spec[i * ch : (i + 1) * ch, r * ch : (r + 1) * ch]
+    owners = small_ref.shape[0]
+    part = 2 * ch // owners
+    rows = ch // owners
+    for o in range(owners):
+        side, row = divmod(o, owners // 2)
+        at = slice(row * part, (row + 1) * part)
+        lanes = slice(side * 2 * ch, (side + 1) * 2 * ch)
+        up_ref[at, lanes] = small_ref[o, :part]
+        down_ref[at, lanes] = small_ref[o, part : 2 * part]
+        skip_ref[o * rows : (o + 1) * rows] = small_ref[o, 2 * part : 2 * part + rows, :ch]
 
 
 def twice(weight):
@@ -428,22 +446,25 @@
     cell_scale = 1.0 / math.sqrt(length_x * all_pencils)
     pencil_scale = 1.0 / math.sqrt(all_pencils)
     at = kept * ch
-    part = 2 * ch // owners
     everyone = lambda axis: [list(range(lax.axis_size(axis)))]
     small = to_group(total[at:], "gy", everyone("gy"))
     spec = total[:at]
     spec = spec + swapped(spec, "gy", 1)
     small = jnp.sum(small, axis=0) * cell_scale
     small = to_group(small, "gz", everyone("gz"))
-    spec = (spec + swapped(spec, "gy", 2) + swapped(spec, "gy", 4) + swapped(spec, "gy", 6)) * pencil_scale
-    grad_spec = spec.reshape(kept, ch, 2, ch).transpose(0, 2, 1, 3)
-
-    def joined(block):
-        return block.reshape(2, ch, 2 * ch).transpose(1, 0, 2).reshape(ch, hid)
-
-    grad_up = joined(small[:, :part])
-    grad_down = joined(small[:, part : 2 * part]).T
-    grad_skip = small[:, 2 * part : 2 * part + ch // owners, :ch].reshape(ch, ch)
+    parts = [spec] + [swapped(spec, "gy", mask) for mask in (2, 4, 6)]
+    grad_spec, grad_skip, grad_up, down_t = pl.pallas_call(
+        lambda *refs: unpack_kernel(pencil_scale, *refs),
+        out_shape=[
+            jax.ShapeDtypeStruct((kept, 2, ch, ch), F32),
+            jax.ShapeDtypeStruct((ch, ch), F32),
+            jax.ShapeDtypeStruct((ch, hid), F32),
+            jax.ShapeDtypeStruct((ch, hid), F32),
+        ],
+        compiler_params=pltpu.CompilerParams(vmem_limit_bytes=8 << 20),
+        name="unpack",
+    )(*parts, small)
+    grad_down = down_t.T
 
     def unpacked(x):
         return x.reshape(count_y, count_z, ch, length_x).transpose(3, 0, 1, 2)

time: 122 us -> 116 us (0.951)
  waiting for transfers between devices: 21.9 us -> 5.81 us
  blocking collectives: 15.1 us -> 28.5 us
  local copies, waits for them, and re-layouts: 5.15 us -> 2.4 us
    all_to_all x0 -> x1, blocking collectives: none -> 13.4 us  [local(): lax.all_to_all(chip_sum, 'gz', 0, 0, axis_index_groups=same_core, tiled=T...]
    all_to_all x1 -> x0, waiting for transfers between devices: 11.2 us -> none  [local(): lax.all_to_all(chip_sum, 'gz', 0, 0, axis_index_groups=same_core, tiled=T...]
    all_to_all x2, waiting for transfers between devices: 8.69 us -> 3.76 us  [to_group(): lax.all_to_all(jnp.broadcast_to(block[None], (peers, *block.shape)), axis...]
    all_to_all x1 -> x0, starting transfers between devices: 3.54 us -> none  [local(): lax.all_to_all(chip_sum, 'gz', 0, 0, axis_index_groups=same_core, tiled=T...]
    all_to_all x2, starting transfers between devices: 11 us -> 13.2 us  [to_group(): lax.all_to_all(jnp.broadcast_to(block[None], (peers, *block.shape)), axis...]
    unnamed x15 -> x12, local copies, waits for them, and re-layouts: 2.39 us -> 1.06 us
  transfers between devices with their start and end apart: 9 -> 8, of which waited for: 4 -> 2; matrix products, arithmetic and copies ran while one was open for 2% -> 1% of each run, Pallas kernels for 16% -> 17%
where the time goes in v5:
time: 116 us; the launch traced here: 115 us
  Pallas kernels  55.3 us (48%)
  blocking collectives  28.5 us (25%)
  starting transfers between devices  22 us (19%)
  waiting for transfers between devices  5.81 us (5%)
  local copies, waits for them, and re-layouts  2.4 us (2%)
    pallas_call x1, Pallas kernels, local(): pl.pallas_call(main_kernel, grid=(pairs // PER_STEP,), in_specs=[smem, wh...  33.4 us
    all_to_all x1, blocking collectives, local(): lax.all_to_all(copies, 'gz', 0, 0, axis_index_groups=same_core, tiled=True)  15.1 us
    all_to_all x1, blocking collectives, local(): lax.all_to_all(chip_sum, 'gz', 0, 0, axis_index_groups=same_core, tiled=T...  13.4 us
    all_to_all x2, starting transfers between devices, to_group(): lax.all_to_all(jnp.broadcast_to(block[None], (peers, *block.shape)), axis...  13.2 us
    pallas_call x1, Pallas kernels, local(): pl.pallas_call(pre_kernel, grid=(pairs // PRE_STEP,), in_specs=[big(PRE_S...  12.2 us
    ppermute x6, starting transfers between devices, swapped(): lax.ppermute(block, axis, [(i, i ^ mask) for i in range(lax.axis_size(axi...  8.81 us
    pallas_call x1, Pallas kernels, local(): pl.pallas_call(final_kernel, grid=(pairs // FINAL_STEP,), in_specs=[smem,...  7.11 us
    all_to_all x2, waiting for transfers between devices, to_group(): lax.all_to_all(jnp.broadcast_to(block[None], (peers, *block.shape)), axis...  3.76 us
  transfers between devices with their start and end apart: 8, of which 2 were waited for; matrix products, arithmetic and copies ran while one was open for 1% of the time, Pallas kernels for 17%

profile of v5, /device:TPU:1, one launch (start us, length us, event | category | flops | bytes accessed | tf_op | source)
XLA Modules:
  0.0 114.9 jit_solution(4164575338196201104)
XLA Ops:
  0.6 1.8 %copies.1 = f32[8,128,128]{2,1,0:T(8,128)} custom-call(f32[2,2,64,64]{3,2,1,0:T(8,128)} %w_ref.1), custom_call_target="tpu_custom_call" | custom-call | tf_op jit(solution)/shard_map/copies/pallas_call | solution.py:341
  2.4 15.1 %all_to_all.20.mine_ref = f32[8,128,128]{2,1,0:T(8,128)S(1)} all-to-all(f32[8,128,128]{2,1,0:T(8,128)} %copies.1), channel_id=1, replica_groups={{0,2,4,6,8,10,12,14},{1,3,5,7,9,11,13,15},{16,18,20,22,24,26,28,30},{17..., dimensions={0} | all-to-all | bytes 1048576 | tf_op jit(solution)/shard_map/all_to_all | solution.py:346
  17.5 1.8 %collective-permute-start = (f32[8,128,128]{2,1,0:T(8,128)S(1)}, f32[8,128,128]{2,1,0:T(8,128)S(1)}, u32[]{:S(2)}, u32[]{:S(2)}) collective-permute-start(f32[8,128,128]{2,1,0:T(8,128)S(1)} %all_to_all.20.mine_ref), channel_id=1, source_target_pairs={{0,1},{1,0},{2,3},{3,2},{4,5},{5,4},{6,7},{7,6},{8,9},{9,8},{10,11... | collective-permute-start | bytes 1572872 | tf_op jit(solution)/shard_map/ppermute | solution.py:35
  19.3 12.2 %pre.1 = (f32[16,64,128]{2,1,0:T(8,128)}, bf16[16,512,1024]{2,1,0:T(8,128)(2,1)}) custom-call(bf16[16,128,1024]{2,1,0:T(8,128)(2,1)} %bitcast.20, bf16[16,128,1024]{2,1,0:T(8,128)(2,1)} %bitcast.22, bf16[1024,64]{1,0:T(8,128)(2,1)} %constant.29.clone.ana_ref, bf16[64,256]{1,0:T(8,128)(2,1)} %bitcast.16), custom_call_target="tpu_custom_call" | custom-call | flops 1342177280 | bytes 25165824 | tf_op jit(solution)/shard_map/pre/pallas_call | solution.py:354
  31.5 0.0 collective-permute-done.other_ref
  31.5 0.0 copy-done.2
  31.5 0.0 copy-done.4
  31.6 0.0 copy-done.5
  31.6 0.0 copy-start.3
  31.6 1.0 copy-done.3
  32.6 33.4 %main.1 = (bf16[16,128,1024]{2,1,0:T(8,128)(2,1)}, bf16[16,128,1024]{2,1,0:T(8,128)(2,1)}, f32[8,152,128]{2,1,0:T(8,128)S(1)}, f32[8,152,128]{2,1,0:T(8,128)S(1)}, f32[1024,128]{1,0:T(8,128)S(1)}) custom-call(s32[1]{0:T(128)} %bitcast.core_ref, f32[1024,128]{1,0:T(8,128)S(1)} %bitcast.18, f32[8,128,128]{2,1,0:T(8,128)S(1)} %all_to_all.20.mine_ref, ...), custom_call_target="tpu_custom_call" | custom-call | flops 8589934592 | bytes 33554432 | tf_op jit(solution)/shard_map/main/pallas_call | solution.py:377
  66.0 0.0 collective-permute-start.1
  66.0 2.0 %collective-permute-done.1 = f32[8,152,128]{2,1,0:T(8,128)S(1)} collective-permute-done((f32[8,152,128]{2,1,0:T(8,128)S(1)}, f32[8,152,128]{2,1,0:T(8,128)S(1)}, u32[]{:S(2)}, u32[]{:S(2)}) %collective-permute-start.1) | collective-permute-done | bytes 622624 | tf_op jit(solution)/shard_map/ppermute | solution.py:35
  68.1 0.1 add.15
  68.1 13.4 %all_to_all.21 = f32[8,152,128]{2,1,0:T(8,128)S(1)} all-to-all(f32[8,152,128]{2,1,0:T(8,128)S(1)} %add.15), channel_id=1, replica_groups={{0,2,4,6,8,10,12,14},{1,3,5,7,9,11,13,15},{16,18,20,22,24,26,28,30},{17..., dimensions={0} | all-to-all | bytes 1245184 | tf_op jit(solution)/shard_map/all_to_all | solution.py:420
  81.6 0.6 broadcast_in_dim.7
  82.3 7.4 %all-to-all-start.2 = ((f32[8,24,128]{2,1,0:T(8,128)}), f32[8,24,128]{2,1,0:T(8,128)S(1)}, u32[]{:S(2)}, u32[]{:S(2)}) async-start(f32[8,24,128]{2,1,0:T(8,128)} %broadcast_in_dim.7), calls=%async_computation.2 | async-start | bytes 196608 | tf_op jit(solution)/shard_map/all_to_all | solution.py:28
  89.6 0.1 fusion.2.skip_ref
  89.7 3.0 %collective-permute-start.2 = (f32[128,128]{1,0:T(8,128)S(1)}, f32[128,128]{1,0:T(8,128)S(1)}, u32[]{:S(2)}, u32[]{:S(2)}) collective-permute-start(f32[128,128]{1,0:T(8,128)S(1)} %slice.8), channel_id=1, source_target_pairs={{0,16},{16,0},{32,48},{48,32},{64,80},{80,64},{96,112},{112,96},{1... | collective-permute-start | bytes 196616 | tf_op jit(solution)/shard_map/ppermute | solution.py:35
  92.8 3.8 %all-to-all-done.2 = f32[8,24,128]{2,1,0:T(8,128)S(1)} async-done(((f32[8,24,128]{2,1,0:T(8,128)}), f32[8,24,128]{2,1,0:T(8,128)S(1)}, u32[]{:S(2)}, u32[]{:S(2)}) %all-to-all-start.2) | async-done | bytes 98336 | tf_op jit(solution)/shard_map/all_to_all | solution.py:28
  96.6 0.7 broadcast_in_dim.8
  97.2 5.8 %all-to-all-start.3 = ((f32[16,24,128]{2,1,0:T(8,128)}), f32[16,24,128]{2,1,0:T(8,128)S(1)}, u32[]{:S(2)}, u32[]{:S(2)}) async-start(f32[16,24,128]{2,1,0:T(8,128)} %broadcast_in_dim.8), calls=%async_computation.3 | async-start | bytes 393216 | tf_op jit(solution)/shard_map/all_to_all | solution.py:28
  103.1 0.0 collective-permute-done.2
  103.1 0.3 collective-permute-start.3
  103.3 1.8 %collective-permute-start.4 = (f32[128,128]{1,0:T(8,128)S(1)}, f32[128,128]{1,0:T(8,128)S(1)}, u32[]{:S(2)}, u32[]{:S(2)}) collective-permute-start(f32[128,128]{1,0:T(8,128)S(1)} %slice_add_fusion.refs_0_), channel_id=1, source_target_pairs={{0,64},{16,80},{32,96},{48,112},{64,0},{80,16},{96,32},{112,48},{1... | collective-permute-start | bytes 196616 | tf_op jit(solution)/shard_map/ppermute | solution.py:35
  105.1 1.9 %collective-permute-start.5 = (f32[128,128]{1,0:T(8,128)S(1)}, f32[128,128]{1,0:T(8,128)S(1)}, u32[]{:S(2)}, u32[]{:S(2)}) collective-permute-start(f32[128,128]{1,0:T(8,128)S(1)} %slice_add_fusion.refs_0_), channel_id=1, source_target_pairs={{0,96},{16,112},{32,64},{48,80},{64,32},{80,48},{96,0},{112,16},{1... | collective-permute-start | bytes 196616 | tf_op jit(solution)/shard_map/ppermute | solution.py:35
  107.0 7.1 %final.1 = bf16[16,128,1024]{2,1,0:T(8,128)(2,1)} custom-call(s32[1]{0:T(128)} %bitcast.core_ref, f32[1024,128]{1,0:T(8,128)S(1)} %get-tuple-element.20.c_ref, f32[8,128,128]{2,1,0:T(8,128)S(1)} %all_to_all.20.mine_ref, f32[8,128,128]{2,1,0:T(8,128)S(1)} %collective-permute-done.other_ref, bf16[16,128,1024]{2,1,0:T(8,128)(2,1)} %get-tuple-element.21.pg_ref, ...), custom_call_target="tpu_custom_call" | custom-call | flops 1073741824 | bytes 8388608 | tf_op jit(solution)/shard_map/final/pallas_call | solution.py:422
  114.1 0.0 collective-permute-done.3.refs_1_
  114.1 0.0 collective-permute-done.4.refs_2_
  114.1 0.0 collective-permute-done.5.refs_3_
  114.1 0.0 all-to-all-done.3.refs_4_
  114.2 0.7 unpack.1
  (13 shorter events, 0.1 us)
Async XLA Ops:
  17.5 14.0 %collective-permute-start = (f32[8,128,128]{2,1,0:T(8,128)S(1)}, f32[8,128,128]{2,1,0:T(8,128)S(1)}, u32[]{:S(2)}, u32[]{:S(2)}) collective-permute-start(f32[8,128,128]{2,1,0:T(8,128)S(1)} %all_to_all.20.mine_ref), channel_id=1, source_target_pairs={{0,1},{1,0},{2,3},{3,2},{4,5},{5,4},{6,7},{7,6},{8,9},{9,8},{10,11... | collective-permute-start | bytes 1572872 | tf_op jit(solution)/shard_map/ppermute | solution.py:35
  19.3 12.2 %copy-start.1 = (bf16[256,64]{0,1:T(8,128)(2,1)S(1)}, bf16[256,64]{0,1:T(8,128)(2,1)}, u32[]{:S(2)}) copy-start(bf16[256,64]{0,1:T(8,128)(2,1)} %param.13) | copy-start | bytes 98308
  19.3 12.2 %copy-start.2 = (bf16[64,64]{1,0:T(8,128)(2,1)S(1)}, bf16[64,64]{1,0:T(8,128)(2,1)}, u32[]{:S(2)}) copy-start(bf16[64,64]{1,0:T(8,128)(2,1)} %skip_ref.1) | copy-start | bytes 24580
  19.3 12.2 %copy-start.4 = (bf16[64,256]{1,0:T(8,128)(2,1)S(1)}, bf16[64,256]{1,0:T(8,128)(2,1)}, u32[]{:S(2)}) copy-start(bf16[64,256]{1,0:T(8,128)(2,1)} %up_ref.1) | copy-start | bytes 98308
  19.3 12.2 %copy-start.5 = (bf16[64,1024]{1,0:T(8,128)(2,1)S(1)}, bf16[64,1024]{1,0:T(8,128)(2,1)}, u32[]{:S(2)}) copy-start(bf16[64,1024]{1,0:T(8,128)(2,1)} %constant.30.clone.syn_ref) | copy-start | bytes 393220
  31.6 1.0 copy-start.3
  66.0 41.0 %copy-start = (bf16[64,1024]{1,0:T(8,128)(2,1)S(1)}, bf16[64,1024]{1,0:T(8,128)(2,1)}, u32[]{:S(2)}) copy-start(bf16[64,1024]{1,0:T(8,128)(2,1)} %constant.31.clone.ana_ref) | copy-start | bytes 393220
  66.0 2.1 %collective-permute-start.1 = (f32[8,152,128]{2,1,0:T(8,128)S(1)}, f32[8,152,128]{2,1,0:T(8,128)S(1)}, u32[]{:S(2)}, u32[]{:S(2)}) collective-permute-start(f32[8,152,128]{2,1,0:T(8,128)S(1)} %get-tuple-element.23), channel_id=1, source_target_pairs={{0,1},{1,0},{2,3},{3,2},{4,5},{5,4},{6,7},{7,6},{8,9},{9,8},{10,11... | collective-permute-start | bytes 1867784 | tf_op jit(solution)/shard_map/ppermute | solution.py:35
  82.3 14.3 %all-to-all-start.2 = ((f32[8,24,128]{2,1,0:T(8,128)}), f32[8,24,128]{2,1,0:T(8,128)S(1)}, u32[]{:S(2)}, u32[]{:S(2)}) async-start(f32[8,24,128]{2,1,0:T(8,128)} %broadcast_in_dim.7), calls=%async_computation.2 | async-start | bytes 196608 | tf_op jit(solution)/shard_map/all_to_all | solution.py:28
  89.7 13.3 %collective-permute-start.2 = (f32[128,128]{1,0:T(8,128)S(1)}, f32[128,128]{1,0:T(8,128)S(1)}, u32[]{:S(2)}, u32[]{:S(2)}) collective-permute-start(f32[128,128]{1,0:T(8,128)S(1)} %slice.8), channel_id=1, source_target_pairs={{0,16},{16,0},{32,48},{48,32},{64,80},{80,64},{96,112},{112,96},{1... | collective-permute-start | bytes 196616 | tf_op jit(solution)/shard_map/ppermute | solution.py:35
  97.2 16.9 %all-to-all-start.3 = ((f32[16,24,128]{2,1,0:T(8,128)}), f32[16,24,128]{2,1,0:T(8,128)S(1)}, u32[]{:S(2)}, u32[]{:S(2)}) async-start(f32[16,24,128]{2,1,0:T(8,128)} %broadcast_in_dim.8), calls=%async_computation.3 | async-start | bytes 393216 | tf_op jit(solution)/shard_map/all_to_all | solution.py:28
  103.1 11.1 %collective-permute-start.3 = (f32[128,128]{1,0:T(8,128)S(1)}, f32[128,128]{1,0:T(8,128)S(1)}, u32[]{:S(2)}, u32[]{:S(2)}) collective-permute-start(f32[128,128]{1,0:T(8,128)S(1)} %slice_add_fusion.refs_0_), channel_id=1, source_target_pairs={{0,32},{16,48},{32,0},{48,16},{64,96},{80,112},{96,64},{112,80},{1... | collective-permute-start | bytes 196616 | tf_op jit(solution)/shard_map/ppermute | solution.py:35
  103.3 10.8 %collective-permute-start.4 = (f32[128,128]{1,0:T(8,128)S(1)}, f32[128,128]{1,0:T(8,128)S(1)}, u32[]{:S(2)}, u32[]{:S(2)}) collective-permute-start(f32[128,128]{1,0:T(8,128)S(1)} %slice_add_fusion.refs_0_), channel_id=1, source_target_pairs={{0,64},{16,80},{32,96},{48,112},{64,0},{80,16},{96,32},{112,48},{1... | collective-permute-start | bytes 196616 | tf_op jit(solution)/shard_map/ppermute | solution.py:35
  105.1 9.0 %collective-permute-start.5 = (f32[128,128]{1,0:T(8,128)S(1)}, f32[128,128]{1,0:T(8,128)S(1)}, u32[]{:S(2)}, u32[]{:S(2)}) collective-permute-start(f32[128,128]{1,0:T(8,128)S(1)} %slice_add_fusion.refs_0_), channel_id=1, source_target_pairs={{0,96},{16,112},{32,64},{48,80},{64,32},{80,48},{96,0},{112,16},{1... | collective-permute-start | bytes 196616 | tf_op jit(solution)/shard_map/ppermute | solution.py:35
